TPU v7x, 32 devices: a whole 2x2x4 slice. The times are simulated.
32 devices in a mesh: groups: 2 (over y), expert: 4 (over z), section: 4 (over x, core).
Axes of the slice: x: 2, y: 2, z: 4, core: 2. Of those that a mesh axis runs over, the one named last changes fastest.
Arguments:
- pending_microgroups: bfloat16 [4, 1024, 768], P('section', ('groups', 'expert')), parts along dimension 1, may hold values from -6 to 6
- arriving_microgroups: bfloat16 [2, 1024, 768], P(None, ('groups', 'expert')), parts along dimension 1, may hold values from -6 to 6
- expert_choice_grid: int32 [3, 4, 1024], P(None, 'section', ('groups', 'expert')), parts along dimension 2, may hold values from 0 to 1, as said below
- rootmean_gain: float32 [4, 768], P('section'), may hold values from 0.5 to 1.5
- gating_columns: bfloat16 [4, 768, 2], P('section'), may hold values from -0.21875 to 0.21875
- up_projection_matrix: bfloat16 [4, 4, 768, 768], P('section', 'expert'), may hold values from -0.21875 to 0.21875
- down_projection_matrix: bfloat16 [4, 4, 768, 768], P('section', 'expert'), may hold values from -0.21875 to 0.21875
Outputs:
- section_out: bfloat16 [4, 3, 1024, 768], P('section', None, ('groups', 'expert')), parts along dimension 2
There are 2 independent parts, one for each index of `groups`. A program takes and returns all parts, laid end to end along the dimension named above; an argument that names none is the same for every part. Nothing has to cross between parts.
Inputs may be any that keep to these rules, and one draw needn't show every extreme that they name: `expert_choice_grid`: for every tick and section, no expert is named by more than 128 tokens of one aligned block of 128 tokens (the tokens of one device), and one expert, drawn from the seed, is named by exactly 128 tokens of every such block.
All inputs are finite; a program needn't handle non-finite values.
Results may differ from a plain program's by a relative error of at most 0.0095.
Values may be sent and summed in bfloat16 or wider, within the bound.
No kernel may reach another device: no remote copies, remote signals or barrier semaphores. Data moves between devices by JAX's collectives and lax.ppermute only.
A program may use at most 64 MiB of HBM per device.

v0:
```python
import functools

import jax
import jax.numpy as jnp
from jax import lax
from jax.experimental import pallas as pl
from jax.experimental.pallas import tpu as pltpu
from jax.sharding import PartitionSpec as P


TICKS = 3


def swapped(x, axis, bit):
    return lax.ppermute(x, axis, [(i, i ^ 1 << bit) for i in range(lax.axis_size(axis))])


def from_behind(value, axis, steps):
    count = lax.axis_size(axis)
    initial, last = (max(0, -steps), min(count, count - steps))
    return lax.ppermute(value, axis, [(source, source + steps) for source in range(initial, last)])


def half_output(received, up_projection_matrix, down_projection_matrix):
    hidden = jnp.maximum(
        jnp.einsum(
            "sid,dh->sih", received, up_projection_matrix, preferred_element_type=jnp.float32
        ),
        0.0,
    ).astype(jnp.bfloat16)
    return jnp.einsum(
        "sih,hd->sid", hidden, down_projection_matrix, preferred_element_type=jnp.float32
    ).astype(jnp.bfloat16)


def expert_layer(
    tok_rows,
    routes,
    rootmean_gain,
    gating_columns,
    up_projection_matrix,
    down_projection_matrix,
    other_in,
    other_out,
):
    num_rows, width = tok_rows.shape
    experts = gating_columns.shape[1]
    capacity = min(num_rows, 3 * num_rows // experts)
    float_rows = tok_rows.astype(jnp.float32)
    inv_rms = lax.rsqrt(jnp.mean(float_rows * float_rows, axis=-1, keepdims=True) + 1e-06)
    normed = (float_rows * inv_rms * rootmean_gain).astype(jnp.bfloat16)
    logits = jnp.dot(normed, gating_columns, preferred_element_type=jnp.float32)
    one_hot = routes[:, None] == jnp.arange(experts, dtype=jnp.int32)[None, :]
    gate_value = jax.nn.sigmoid(jnp.sum(jnp.where(one_hot, logits, 0.0), axis=1))
    flags = one_hot.astype(jnp.int32)
    slot_rank = jnp.sum((jnp.cumsum(flags, axis=0) - flags) * flags, axis=1)
    slot_index = routes * capacity + slot_rank
    placing = (
        slot_index[None, :] == jnp.arange(experts * capacity, dtype=jnp.int32)[:, None]
    ).astype(jnp.bfloat16)
    outgoing = jnp.dot(placing, normed, preferred_element_type=jnp.float32).astype(jnp.bfloat16)
    outgoing = outgoing.reshape(experts, capacity, width)
    halves = outgoing.reshape(2 * experts, capacity // 2, width)
    received = lax.all_to_all(halves, "expert", split_axis=0, concat_axis=0, tiled=True)
    own_part = half_output(received, up_projection_matrix, down_projection_matrix)
    other_part = half_output(received, other_in, other_out)
    summed = (own_part.astype(jnp.float32) + other_part.astype(jnp.float32)).astype(jnp.bfloat16)
    combined = lax.all_to_all(summed, "expert", split_axis=0, concat_axis=0, tiled=True)
    flat_out = combined.reshape(experts * capacity, width)
    expert_out = lax.dot_general(
        placing, flat_out, (((0,), (0,)), ((), ())), preferred_element_type=jnp.float32
    )
    return (float_rows + gate_value[:, None] * expert_out).astype(jnp.bfloat16)


def slots_per_device(
    pending_microgroups,
    arriving_microgroups,
    expert_choice_grid,
    rootmean_gain,
    gating_columns,
    up_projection_matrix,
    down_projection_matrix,
):
    leg_position = lax.axis_index("section")
    own_in = up_projection_matrix[0, 0]
    own_out = down_projection_matrix[0, 0]
    other_in, other_out = swapped((own_in, own_out), "expert", 0)
    running_activation = pending_microgroups[0]
    per_tick = []
    for tick_idx in range(TICKS):
        layer_out = expert_layer(
            running_activation,
            expert_choice_grid[tick_idx, 0],
            rootmean_gain[0],
            gating_columns[0],
            own_in,
            own_out,
            other_in,
            other_out,
        )
        per_tick.append(layer_out)
        if tick_idx + 1 < TICKS:
            moved = from_behind(layer_out, "section", 1)
            running_activation = jnp.where(leg_position == 0, arriving_microgroups[tick_idx], moved)
    return jnp.stack(per_tick)[None]


def piece_list(width):
    third, half = width // 3, width // 6
    return [
        (0, 0, half, half + third),
        (0, half, third, half + third),
        (1, 0, third, third),
        (1, 2 * third, third, 0),
    ]


def cut_kernel(some, *refs):
    count = len(some)
    sources, outs, sems = refs[: -count - 1], refs[-count - 1 : -1], refs[-1]
    group = lax.axis_index("groups")
    copies = []
    for index, ((m, first, size, share), out) in enumerate(zip(some, outs)):
        rows = pl.ds(pl.multiple_of(group * share + first, 128), size)
        copies.append(pltpu.make_async_copy(sources[m].at[rows, :], out, sems.at[index]))
    for copy in copies:
        copy.start()
    for copy in copies:
        copy.wait()


def join_kernel(some, *refs):
    refs, out_ref = list(refs[:-1]), refs[-1]
    group = lax.axis_index("groups")
    for _, first, size, share in some:
        for part in (group, 1 - group) if share else (0,):
            rows = pl.ds(pl.multiple_of(part * share + first, 128), size)
            out_ref[rows, :] = refs.pop(0)[...]


def from_pieces(rows, some, refs):
    refs = list(refs)
    group = lax.axis_index("groups")
    total = 0.0
    for _, first, size, share in some:
        taken = [rows[:, first : first + size]]
        if share:
            other = rows[:, share + first : share + first + size]
            taken = [jnp.where(group == 0, *pair) for pair in ((*taken, other), (other, *taken))]
        for part in taken:
            total += jnp.dot(part, refs.pop(0)[...], preferred_element_type=jnp.float32)
    return total


def layer_kernel(tick, which, last_tick, some, *refs):
    refs = list(refs)
    take = refs.pop
    routes_ref = take(0)
    straight_ref = take(0)
    cross_ref = take(0) if tick else None
    fresh_ref = take(0) if which == 0 else None
    gain_ref, columns_ref, up_ref, down_ref, far_up_ref = [take(0) for _ in range(5)]
    far_down_refs = [take(0) for _ in range(1 if tick else sum(2 if p[3] else 1 for p in some))]
    take(0)
    y_ref = take(0)
    side = lax.axis_index("expert") // 2
    leg = lax.axis_index("section")
    x = straight_ref[...].astype(jnp.float32)
    if tick:
        x = x + cross_ref[...].astype(jnp.float32)
        if which == 0:
            take(0)[...] = x.astype(jnp.bfloat16)
            x = jnp.where(leg == 0, fresh_ref[tick - 1].astype(jnp.float32), x)
    inv_rms = lax.rsqrt(jnp.mean(x * x, axis=-1, keepdims=True) + 1e-06)
    normed = (x * inv_rms * gain_ref[...]).astype(jnp.bfloat16)
    columns = columns_ref[...].astype(jnp.float32)
    column = jnp.where(side == 0, columns[0:1], columns[1:2])
    logit = jnp.sum(normed.astype(jnp.float32) * column, axis=-1, keepdims=True)
    gate = jax.nn.sigmoid(logit)
    hidden = []
    for ref in (up_ref, far_up_ref):
        up = jnp.dot(normed, ref[...], preferred_element_type=jnp.float32)
        hidden.append(jnp.maximum(up, 0.0).astype(jnp.bfloat16))
    out = jnp.dot(hidden[0], down_ref[...], preferred_element_type=jnp.float32)
    if len(far_down_refs) == 1:
        out = out + jnp.dot(hidden[1], far_down_refs[0][...], preferred_element_type=jnp.float32)
    else:
        out = out + from_pieces(hidden[1], some, far_down_refs)
    y = x + gate * out
    y = jnp.where(routes_ref[tick, 0, 0] == side, y, 0.0).astype(jnp.bfloat16)
    y_ref[...] = y
    if which == 0 and tick < last_tick:
        take(0)[...] = jnp.where(leg == lax.axis_size("section") - 1, fresh_ref[tick], y)


def gather_kernel(first_ref, second_ref, own_ref, returned_ref, out_ref):
    out_ref[0, 0] = first_ref[...]
    out_ref[0, 1] = second_ref[...]
    total = own_ref[...].astype(jnp.float32) + returned_ref[...].astype(jnp.float32)
    out_ref[0, 2] = total.astype(jnp.bfloat16)


def pairs_per_device(
    pending_microgroups,
    arriving_microgroups,
    expert_choice_grid,
    rootmean_gain,
    gating_columns,
    up_projection_matrix,
    down_projection_matrix,
):
    places = lax.axis_size("expert")
    legs = lax.axis_size("section")
    own = (up_projection_matrix[0, 0], down_projection_matrix[0, 0])
    width, hid = own[0].shape
    num_rows = pending_microgroups.shape[1]
    pieces = piece_list(width)
    in_vmem = pl.BlockSpec(memory_space=pltpu.VMEM)
    anywhere = pl.BlockSpec(memory_space=pl.ANY)
    limited = pltpu.CompilerParams(vmem_limit_bytes=8 << 20)

    def cut(some):
        return pl.pallas_call(
            functools.partial(cut_kernel, some),
            out_shape=[jax.ShapeDtypeStruct((p[2], hid), jnp.bfloat16) for p in some],
            in_specs=[anywhere] * 2,
            out_specs=[CUT_OUT] * len(some),
            scratch_shapes=[pltpu.SemaphoreType.DMA((len(some),))],
            compiler_params=CUT_PARAMS,
        )(*own)

    sending = [*cut(pieces[:1]), *cut(pieces[1:])]
    near, parts = [], {}
    for piece in sending:
        near.append(swapped(piece, "expert", 0))
    for index, piece in enumerate(near):
        parts[index] = [piece]
        if pieces[index][3]:
            parts[index].append(swapped(piece, "groups", 0))
    by_matrix = [[i for i, p in enumerate(pieces) if p[0] == m] for m in (0, 1)]

    def join(m):
        operands = [part for i in by_matrix[m] for part in parts[i]]
        return pl.pallas_call(
            functools.partial(join_kernel, [pieces[i] for i in by_matrix[m]]),
            out_shape=jax.ShapeDtypeStruct((width, hid), jnp.bfloat16),
            in_specs=[in_vmem] * len(operands),
            out_specs=in_vmem,
            compiler_params=limited,
        )(*operands)

    far_up = join(0)
    far_down = join(1)
    down_some = [pieces[i] for i in by_matrix[1]]
    down_parts = [part for i in by_matrix[1] for part in parts[i]]

    columns = jnp.swapaxes(gating_columns[0], 0, 1)
    own_rows = pending_microgroups[0]
    other_rows = swapped(own_rows, "expert", 1)
    rows_shape = jax.ShapeDtypeStruct((num_rows, width), jnp.bfloat16)

    def layer(tick, which, inputs, after):
        operands = [expert_choice_grid, *inputs]
        if which == 0:
            operands.append(arriving_microgroups)
        operands += [rootmean_gain, columns, *own, far_up]
        operands += [far_down] if tick else down_parts
        in_specs = [pl.BlockSpec(memory_space=pltpu.SMEM)] + [in_vmem] * (len(operands) - 1)
        extras = (which == 0) * ((tick > 0) + (tick + 1 < TICKS))
        return pl.pallas_call(
            functools.partial(layer_kernel, tick, which, TICKS - 1, down_some),
            out_shape=[rows_shape] * (1 + extras),
            in_specs=[*in_specs, anywhere],
            out_specs=[in_vmem] * (1 + extras),
            compiler_params=pltpu.CompilerParams(vmem_limit_bytes=16 << 20),
        )(*operands, after)

    def ahead(value, flip, wrap):
        last = legs if wrap else legs - 1
        perm = [
            (e * legs + s, (e ^ flip) * legs + (s + 1) % legs)
            for e in range(places)
            for s in range(last)
        ]
        return lax.ppermute(value, ("expert", "section"), perm)

    def back(value):
        return lax.ppermute(value, "section", [((s + 1) % legs, s) for s in range(legs)])

    current = {0: (own_rows,), 1: (other_rows,)}
    outputs = []
    after = own_rows
    for tick in range(TICKS):
        following = {}
        straight = {}
        done = {}
        for which in chunk_order(tick):
            got = layer(tick, which, current[which], after)
            after = done[which] = got[0]
            if tick + 1 < TICKS:
                following[1 - which] = ahead(got[-1], 2, True)
                straight[which] = ahead(got[0], 0, which == 0)
            elif which == 1:
                returned = swapped(got[0], "expert", 1)
            if tick and which == 0:
                outputs.append(back(got[1]))
        if tick + 1 < TICKS:
            current = {w: (straight[w], following[w]) for w in (0, 1)}
    return pl.pallas_call(
        gather_kernel,
        out_shape=jax.ShapeDtypeStruct((1, TICKS, num_rows, width), jnp.bfloat16),
        in_specs=[in_vmem] * 4,
        out_specs=in_vmem,
        compiler_params=limited,
        name="gather",
    )(*outputs, done[0], returned)


CUT_OUT = pl.BlockSpec(memory_space=pltpu.VMEM)
CUT_PARAMS = pltpu.CompilerParams(vmem_limit_bytes=60 << 20)


def chunk_order(tick):
    return (1, 0) if (TICKS - 1 - tick) % 2 == 0 else (0, 1)


def solution(mesh):
    placed = (
        P("section", ("groups", "expert"), None),
        P(None, ("groups", "expert"), None),
        P(None, "section", ("groups", "expert")),
        P("section", None),
        P("section", None, None),
        P("section", "expert", None, None),
        P("section", "expert", None, None),
    )

    paired = mesh.shape["expert"] == 4 and mesh.shape["groups"] == 2

    def per_device(*args):
        if paired and args[4].shape[2] == 2 and args[5].shape[2] % 768 == 0:
            return pairs_per_device(*args)
        return slots_per_device(*args)

    return jax.shard_map(
        per_device,
        mesh=mesh,
        in_specs=placed,
        out_specs=P("section", None, ("groups", "expert"), None),
        check_vma=False,
    )
```

profile of v0, /device:TPU:0, one launch (start us, length us, event | category | flops | bytes accessed | tf_op | source)
XLA Modules:
  0.0 88.9 jit_solution(7947072406560225970)
XLA Ops:
  0.0 2.3 %shard_map.74 = (bf16[256,768]{1,0:T(8,128)(2,1)}, bf16[256,768]{1,0:T(8,128)(2,1)}, bf16[256,768]{1,0:T(8,128)(2,1)}) custom-call(bf16[768,768]{1,0:T(8,128)(2,1)} %bitcast.6, bf16[768,768]{1,0:T(8,128)(2,1)} %bitcast.14), custom_call_target="tpu_custom_call" | custom-call | tf_op jit(solution)/shard_map/pallas_call | solution.py:224
  2.3 3.1 %collective-permute-start.2 = (bf16[256,768]{1,0:T(8,128)(2,1)}, bf16[256,768]{1,0:T(8,128)(2,1)S(1)}, u32[]{:S(2)}, u32[]{:S(2)}) collective-permute-start(bf16[256,768]{1,0:T(8,128)(2,1)} %get-tuple-element.15), channel_id=1, source_target_pairs={{0,4},{4,0},{8,12},{12,8},{1,5},{5,1},{9,13},{13,9},{2,6},{6,2},{1... | collective-permute-start | bytes 1179656 | tf_op jit(solution)/shard_map/ppermute | solution.py:15
  5.5 1.7 %shard_map.73 = bf16[128,768]{1,0:T(8,128)(2,1)} custom-call(bf16[768,768]{1,0:T(8,128)(2,1)} %bitcast.7, bf16[768,768]{1,0:T(8,128)(2,1)} %bitcast.15), custom_call_target="tpu_custom_call" | custom-call | tf_op jit(solution)/shard_map/pallas_call | solution.py:224
  7.2 1.9 %collective-permute-start = (bf16[128,768]{1,0:T(8,128)(2,1)}, bf16[128,768]{1,0:T(8,128)(2,1)S(1)}, u32[]{:S(2)}, u32[]{:S(2)}) collective-permute-start(bf16[128,768]{1,0:T(8,128)(2,1)} %shard_map.73), channel_id=1, source_target_pairs={{0,4},{4,0},{8,12},{12,8},{1,5},{5,1},{9,13},{13,9},{2,6},{6,2},{1... | collective-permute-start | bytes 589832 | tf_op jit(solution)/shard_map/ppermute | solution.py:15
  9.2 6.4 %collective-permute-done.2.refs_2_ = bf16[256,768]{1,0:T(8,128)(2,1)S(1)} collective-permute-done((bf16[256,768]{1,0:T(8,128)(2,1)}, bf16[256,768]{1,0:T(8,128)(2,1)S(1)}, u32[]{:S(2)}, u32[]{:S(2)}) %collective-permute-start.2) | collective-permute-done | bytes 393248 | tf_op jit(solution)/shard_map/ppermute | solution.py:15
  15.6 2.0 %collective-permute-start.3 = (bf16[256,768]{1,0:T(8,128)(2,1)S(1)}, bf16[256,768]{1,0:T(8,128)(2,1)S(1)}, u32[]{:S(2)}, u32[]{:S(2)}) collective-permute-start(bf16[256,768]{1,0:T(8,128)(2,1)S(1)} %collective-permute-done.2.refs_2_), channel_id=1, source_target_pairs={{0,16},{16,0},{1,17},{17,1},{2,18},{18,2},{3,19},{19,3},{4,20},{20... | collective-permute-start | bytes 1179656 | tf_op jit(solution)/shard_map/ppermute | solution.py:15
  19.1 4.9 %collective-permute-done.4.refs_7_.refs_8_.refs_0_ = bf16[256,768]{1,0:T(8,128)(2,1)S(1)} collective-permute-done((bf16[256,768]{1,0:T(8,128)(2,1)}, bf16[256,768]{1,0:T(8,128)(2,1)S(1)}, u32[]{:S(2)}, u32[]{:S(2)}) %collective-permute-start.4) | collective-permute-done | bytes 393248 | tf_op jit(solution)/shard_map/ppermute | solution.py:15
  24.0 2.0 %collective-permute-start.5 = (bf16[256,768]{1,0:T(8,128)(2,1)S(1)}, bf16[256,768]{1,0:T(8,128)(2,1)S(1)}, u32[]{:S(2)}, u32[]{:S(2)}) collective-permute-start(bf16[256,768]{1,0:T(8,128)(2,1)S(1)} %collective-permute-done.4.refs_7_.refs_8_.refs_0_), channel_id=1, source_target_pairs={{0,16},{16,0},{1,17},{17,1},{2,18},{18,2},{3,19},{19,3},{4,20},{20... | collective-permute-start | bytes 1179656 | tf_op jit(solution)/shard_map/ppermute | solution.py:15
  26.0 2.2 %collective-permute-done.refs_0_ = bf16[128,768]{1,0:T(8,128)(2,1)S(1)} collective-permute-done((bf16[128,768]{1,0:T(8,128)(2,1)}, bf16[128,768]{1,0:T(8,128)(2,1)S(1)}, u32[]{:S(2)}, u32[]{:S(2)}) %collective-permute-start) | collective-permute-done | bytes 196640 | tf_op jit(solution)/shard_map/ppermute | solution.py:15
  28.2 2.0 %collective-permute-start.1 = (bf16[128,768]{1,0:T(8,128)(2,1)S(1)}, bf16[128,768]{1,0:T(8,128)(2,1)S(1)}, u32[]{:S(2)}, u32[]{:S(2)}) collective-permute-start(bf16[128,768]{1,0:T(8,128)(2,1)S(1)} %collective-permute-done.refs_0_), channel_id=1, source_target_pairs={{0,16},{16,0},{1,17},{17,1},{2,18},{18,2},{3,19},{19,3},{4,20},{20... | collective-permute-start | bytes 589832 | tf_op jit(solution)/shard_map/ppermute | solution.py:15
  30.2 2.7 %collective-permute-start.7 = (bf16[128,768]{1,0:T(8,128)(2,1)S(1)}, bf16[128,768]{1,0:T(8,128)(2,1)S(1)}, u32[]{:S(2)}, u32[]{:S(2)}) collective-permute-start(bf16[128,768]{1,0:T(8,128)(2,1)S(1)} %bitcast.22), channel_id=1, source_target_pairs={{0,8},{4,12},{8,0},{12,4},{1,9},{5,13},{9,1},{13,5},{2,10},{6,14},... | collective-permute-start | bytes 589832 | tf_op jit(solution)/shard_map/ppermute | solution.py:15
  32.9 4.8 %collective-permute-done.1.refs_1_ = bf16[128,768]{1,0:T(8,128)(2,1)S(1)} collective-permute-done((bf16[128,768]{1,0:T(8,128)(2,1)S(1)}, bf16[128,768]{1,0:T(8,128)(2,1)S(1)}, u32[]{:S(2)}, u32[]{:S(2)}) %collective-permute-start.1) | collective-permute-done | bytes 196640 | tf_op jit(solution)/shard_map/ppermute | solution.py:15
  44.7 2.6 %collective-permute-start.8 = (bf16[128,768]{1,0:T(8,128)(2,1)S(1)}, bf16[128,768]{1,0:T(8,128)(2,1)S(1)}, u32[]{:S(2)}, u32[]{:S(2)}) collective-permute-start(bf16[128,768]{1,0:T(8,128)(2,1)S(1)} %get-tuple-element.18.refs_10_), channel_id=1, source_target_pairs={{0,1},{1,2},{2,3},{3,0},{4,5},{5,6},{6,7},{7,4},{8,9},{9,10},{10,1... | collective-permute-start | bytes 589832 | tf_op jit(solution)/shard_map/ppermute | solution.py:286
  47.2 1.9 %collective-permute-start.12 = (bf16[128,768]{1,0:T(8,128)(2,1)S(1)}, bf16[128,768]{1,0:T(8,128)(2,1)S(1)}, u32[]{:S(2)}, u32[]{:S(2)}) collective-permute-start(bf16[128,768]{1,0:T(8,128)(2,1)S(1)} %shard_map.76.refs_11_), channel_id=1, source_target_pairs={{0,1},{1,2},{2,3},{4,5},{5,6},{6,7},{8,9},{9,10},{10,11},{12,13},{... | collective-permute-start | bytes 589832 | tf_op jit(solution)/shard_map/ppermute | solution.py:286
  49.7 4.8 %collective-permute-done.9.refs_2_ = bf16[128,768]{1,0:T(8,128)(2,1)S(1)} collective-permute-done((bf16[128,768]{1,0:T(8,128)(2,1)S(1)}, bf16[128,768]{1,0:T(8,128)(2,1)S(1)}, u32[]{:S(2)}, u32[]{:S(2)}) %collective-permute-start.9) | collective-permute-done | bytes 196640 | tf_op jit(solution)/shard_map/ppermute | solution.py:286
  54.5 1.7 %shard_map.79 = (bf16[128,768]{1,0:T(8,128)(2,1)S(1)}, bf16[128,768]{1,0:T(8,128)(2,1)S(1)}, bf16[128,768]{1,0:T(8,128)(2,1)S(1)}) custom-call(s32[3,1,128]{2,1,0:T(1,128)S(1)} %copy-done.6, bf16[128,768]{1,0:T(8,128)(2,1)S(1)} %collective-permute-done.8.refs_1_, bf16[128,768]{1,0:T(8,128)(2,1)S(1)} %collective-permute-done.9.refs_2_, ...), custom_call_target="tpu_custom_call" | custom-call | tf_op jit(solution)/shard_map/pallas_call | solution.py:271
  56.3 6.6 %collective-permute-done.13.refs_2_ = bf16[128,768]{1,0:T(8,128)(2,1)S(1)} collective-permute-done((bf16[128,768]{1,0:T(8,128)(2,1)S(1)}, bf16[128,768]{1,0:T(8,128)(2,1)S(1)}, u32[]{:S(2)}, u32[]{:S(2)}) %collective-permute-start.13) | collective-permute-done | bytes 196640 | tf_op jit(solution)/shard_map/ppermute | solution.py:286
  66.1 2.2 %collective-permute-start.14 = (bf16[128,768]{1,0:T(8,128)(2,1)S(1)}, bf16[128,768]{1,0:T(8,128)(2,1)S(1)}, u32[]{:S(2)}, u32[]{:S(2)}) collective-permute-start(bf16[128,768]{1,0:T(8,128)(2,1)S(1)} %shard_map.80.refs_9_), channel_id=1, source_target_pairs={{0,9},{1,10},{2,11},{3,8},{4,13},{5,14},{6,15},{7,12},{8,1},{9,2},... | collective-permute-start | bytes 589832 | tf_op jit(solution)/shard_map/ppermute | solution.py:286
  70.5 1.7 %shard_map.81.refs_10_ = bf16[128,768]{1,0:T(8,128)(2,1)S(1)} custom-call(s32[3,1,128]{2,1,0:T(1,128)S(1)} %copy-done.6, bf16[128,768]{1,0:T(8,128)(2,1)S(1)} %collective-permute-done.15.refs_1_, bf16[128,768]{1,0:T(8,128)(2,1)S(1)} %collective-permute-done.16.refs_2_, f32[1,768]{1,0:T(1,128)S(1)} %copy-done.4, bf16[2,768]{1,0:T(2,128)(2,1)S(1)} %bitcast.29, ...), custom_call_target="tpu_custom_call" | custom-call | tf_op jit(solution)/shard_map/pallas_call | solution.py:271
  72.2 2.5 %collective-permute-start.18 = (bf16[128,768]{1,0:T(8,128)(2,1)S(1)}, bf16[128,768]{1,0:T(8,128)(2,1)S(1)}, u32[]{:S(2)}, u32[]{:S(2)}) collective-permute-start(bf16[128,768]{1,0:T(8,128)(2,1)S(1)} %shard_map.81.refs_10_), channel_id=1, source_target_pairs={{0,8},{4,12},{8,0},{12,4},{1,9},{5,13},{9,1},{13,5},{2,10},{6,14},... | collective-permute-start | bytes 589832 | tf_op jit(solution)/shard_map/ppermute | solution.py:15
  74.7 4.6 %collective-permute-done.14.refs_2_ = bf16[128,768]{1,0:T(8,128)(2,1)S(1)} collective-permute-done((bf16[128,768]{1,0:T(8,128)(2,1)S(1)}, bf16[128,768]{1,0:T(8,128)(2,1)S(1)}, u32[]{:S(2)}, u32[]{:S(2)}) %collective-permute-start.14) | collective-permute-done | bytes 196640 | tf_op jit(solution)/shard_map/ppermute | solution.py:286
  79.3 1.7 %shard_map.82 = (bf16[128,768]{1,0:T(8,128)(2,1)S(1)}, bf16[128,768]{1,0:T(8,128)(2,1)S(1)}) custom-call(s32[3,1,128]{2,1,0:T(1,128)S(1)} %copy-done.6, bf16[128,768]{1,0:T(8,128)(2,1)S(1)} %collective-permute-done.11.refs_1_, bf16[128,768]{1,0:T(8,128)(2,1)S(1)} %collective-permute-done.14.refs_2_, bf16[2,128,768]{2,1,0:T(8,128)(2,1)S(1)} %copy-done.2, ...), custom_call_target="tpu_custom_call" | custom-call | tf_op jit(solution)/shard_map/pallas_call | solution.py:271
  81.0 1.9 %collective-permute-start.17 = (bf16[128,768]{1,0:T(8,128)(2,1)S(1)}, bf16[128,768]{1,0:T(8,128)(2,1)S(1)}, u32[]{:S(2)}, u32[]{:S(2)}) collective-permute-start(bf16[128,768]{1,0:T(8,128)(2,1)S(1)} %get-tuple-element.23), channel_id=1, source_target_pairs={{1,0},{2,1},{3,2},{0,3},{5,4},{6,5},{7,6},{4,7},{9,8},{10,9},{11,1... | collective-permute-start | bytes 589832 | tf_op jit(solution)/shard_map/ppermute | solution.py:289
  82.9 5.1 %collective-permute-done.18.returned_ref = bf16[128,768]{1,0:T(8,128)(2,1)S(1)} collective-permute-done((bf16[128,768]{1,0:T(8,128)(2,1)S(1)}, bf16[128,768]{1,0:T(8,128)(2,1)S(1)}, u32[]{:S(2)}, u32[]{:S(2)}) %collective-permute-start.18) | collective-permute-done | bytes 196640 | tf_op jit(solution)/shard_map/ppermute | solution.py:15
  (41 shorter events, 15.5 us)
Async XLA Ops:
  2.3 13.3 %collective-permute-start.2 = (bf16[256,768]{1,0:T(8,128)(2,1)}, bf16[256,768]{1,0:T(8,128)(2,1)S(1)}, u32[]{:S(2)}, u32[]{:S(2)}) collective-permute-start(bf16[256,768]{1,0:T(8,128)(2,1)} %get-tuple-element.15), channel_id=1, source_target_pairs={{0,4},{4,0},{8,12},{12,8},{1,5},{5,1},{9,13},{13,9},{2,6},{6,2},{1... | collective-permute-start | bytes 1179656 | tf_op jit(solution)/shard_map/ppermute | solution.py:15
  5.4 12.1 %copy-start.7 = (bf16[256,768]{1,0:T(8,128)(2,1)S(1)}, bf16[256,768]{1,0:T(8,128)(2,1)}, u32[]{:S(2)}) copy-start(bf16[256,768]{1,0:T(8,128)(2,1)} %get-tuple-element.17) | copy-start | bytes 1179652
  5.4 24.8 %copy-start.3 = (bf16[1,128,768]{2,1,0:T(8,128)(2,1)S(1)}, bf16[1,128,768]{2,1,0:T(8,128)(2,1)}, u32[]{:S(2)}) copy-start(bf16[1,128,768]{2,1,0:T(8,128)(2,1)} %param.7) | copy-start | bytes 589828
  5.4 18.6 %collective-permute-start.4 = (bf16[256,768]{1,0:T(8,128)(2,1)}, bf16[256,768]{1,0:T(8,128)(2,1)S(1)}, u32[]{:S(2)}, u32[]{:S(2)}) collective-permute-start(bf16[256,768]{1,0:T(8,128)(2,1)} %get-tuple-element.16), channel_id=1, source_target_pairs={{0,4},{4,0},{8,12},{12,8},{1,5},{5,1},{9,13},{13,9},{2,6},{6,2},{1... | collective-permute-start | bytes 1179656 | tf_op jit(solution)/shard_map/ppermute | solution.py:15
  5.5 34.5 %copy-start.5 = (bf16[1,768,2]{1,2,0:T(2,128)(2,1)S(1)}, bf16[1,768,2]{1,2,0:T(2,128)(2,1)}, u32[]{:S(2)}) copy-start(bf16[1,768,2]{1,2,0:T(2,128)(2,1)} %param.11) | copy-start | bytes 9220
  5.5 34.5 %copy-start.6 = (s32[3,1,128]{2,1,0:T(1,128)S(1)}, s32[3,1,128]{2,1,0:T(1,128)}, u32[]{:S(2)}) copy-start(s32[3,1,128]{2,1,0:T(1,128)} %refs_0_.11) | copy-start | bytes 4612
  7.2 21.0 %collective-permute-start = (bf16[128,768]{1,0:T(8,128)(2,1)}, bf16[128,768]{1,0:T(8,128)(2,1)S(1)}, u32[]{:S(2)}, u32[]{:S(2)}) collective-permute-start(bf16[128,768]{1,0:T(8,128)(2,1)} %shard_map.73), channel_id=1, source_target_pairs={{0,4},{4,0},{8,12},{12,8},{1,5},{5,1},{9,13},{13,9},{2,6},{6,2},{1... | collective-permute-start | bytes 589832 | tf_op jit(solution)/shard_map/ppermute | solution.py:15
  15.6 22.1 %collective-permute-start.3 = (bf16[256,768]{1,0:T(8,128)(2,1)S(1)}, bf16[256,768]{1,0:T(8,128)(2,1)S(1)}, u32[]{:S(2)}, u32[]{:S(2)}) collective-permute-start(bf16[256,768]{1,0:T(8,128)(2,1)S(1)} %collective-permute-done.2.refs_2_), channel_id=1, source_target_pairs={{0,16},{16,0},{1,17},{17,1},{2,18},{18,2},{3,19},{19,3},{4,20},{20... | collective-permute-start | bytes 1179656 | tf_op jit(solution)/shard_map/ppermute | solution.py:15
  17.5 22.5 %collective-permute-start.6 = (bf16[256,768]{1,0:T(8,128)(2,1)S(1)}, bf16[256,768]{1,0:T(8,128)(2,1)S(1)}, u32[]{:S(2)}, u32[]{:S(2)}) collective-permute-start(bf16[256,768]{1,0:T(8,128)(2,1)S(1)} %copy-done.7), channel_id=1, source_target_pairs={{0,4},{4,0},{8,12},{12,8},{1,5},{5,1},{9,13},{13,9},{2,6},{6,2},{1... | collective-permute-start | bytes 1179656 | tf_op jit(solution)/shard_map/ppermute | solution.py:15
  24.0 16.0 %collective-permute-start.5 = (bf16[256,768]{1,0:T(8,128)(2,1)S(1)}, bf16[256,768]{1,0:T(8,128)(2,1)S(1)}, u32[]{:S(2)}, u32[]{:S(2)}) collective-permute-start(bf16[256,768]{1,0:T(8,128)(2,1)S(1)} %collective-permute-done.4.refs_7_.refs_8_.refs_0_), channel_id=1, source_target_pairs={{0,16},{16,0},{1,17},{17,1},{2,18},{18,2},{3,19},{19,3},{4,20},{20... | collective-permute-start | bytes 1179656 | tf_op jit(solution)/shard_map/ppermute | solution.py:15
  28.2 9.4 %collective-permute-start.1 = (bf16[128,768]{1,0:T(8,128)(2,1)S(1)}, bf16[128,768]{1,0:T(8,128)(2,1)S(1)}, u32[]{:S(2)}, u32[]{:S(2)}) collective-permute-start(bf16[128,768]{1,0:T(8,128)(2,1)S(1)} %collective-permute-done.refs_0_), channel_id=1, source_target_pairs={{0,16},{16,0},{1,17},{17,1},{2,18},{18,2},{3,19},{19,3},{4,20},{20... | collective-permute-start | bytes 589832 | tf_op jit(solution)/shard_map/ppermute | solution.py:15
  30.2 9.9 %copy-start.1 = (bf16[1,1,768,768]{3,2,1,0:T(8,128)(2,1)S(1)}, bf16[1,1,768,768]{3,2,1,0:T(8,128)(2,1)}, u32[]{:S(2)}) copy-start(bf16[1,1,768,768]{3,2,1,0:T(8,128)(2,1)} %param.13) | copy-start | bytes 3538948
  30.2 9.1 %collective-permute-start.7 = (bf16[128,768]{1,0:T(8,128)(2,1)S(1)}, bf16[128,768]{1,0:T(8,128)(2,1)S(1)}, u32[]{:S(2)}, u32[]{:S(2)}) collective-permute-start(bf16[128,768]{1,0:T(8,128)(2,1)S(1)} %bitcast.22), channel_id=1, source_target_pairs={{0,8},{4,12},{8,0},{12,4},{1,9},{5,13},{9,1},{13,5},{2,10},{6,14},... | collective-permute-start | bytes 589832 | tf_op jit(solution)/shard_map/ppermute | solution.py:15
  41.7 12.8 %collective-permute-start.9 = (bf16[128,768]{1,0:T(8,128)(2,1)S(1)}, bf16[128,768]{1,0:T(8,128)(2,1)S(1)}, u32[]{:S(2)}, u32[]{:S(2)}) collective-permute-start(bf16[128,768]{1,0:T(8,128)(2,1)S(1)} %shard_map.76.refs_11_), channel_id=1, source_target_pairs={{0,9},{1,10},{2,11},{3,8},{4,13},{5,14},{6,15},{7,12},{8,1},{9,2},... | collective-permute-start | bytes 589832 | tf_op jit(solution)/shard_map/ppermute | solution.py:286
  44.7 9.9 %collective-permute-start.8 = (bf16[128,768]{1,0:T(8,128)(2,1)S(1)}, bf16[128,768]{1,0:T(8,128)(2,1)S(1)}, u32[]{:S(2)}, u32[]{:S(2)}) collective-permute-start(bf16[128,768]{1,0:T(8,128)(2,1)S(1)} %get-tuple-element.18.refs_10_), channel_id=1, source_target_pairs={{0,1},{1,2},{2,3},{3,0},{4,5},{5,6},{6,7},{7,4},{8,9},{9,10},{10,1... | collective-permute-start | bytes 589832 | tf_op jit(solution)/shard_map/ppermute | solution.py:286
  47.2 9.1 %collective-permute-start.12 = (bf16[128,768]{1,0:T(8,128)(2,1)S(1)}, bf16[128,768]{1,0:T(8,128)(2,1)S(1)}, u32[]{:S(2)}, u32[]{:S(2)}) collective-permute-start(bf16[128,768]{1,0:T(8,128)(2,1)S(1)} %shard_map.76.refs_11_), channel_id=1, source_target_pairs={{0,1},{1,2},{2,3},{4,5},{5,6},{6,7},{8,9},{9,10},{10,11},{12,13},{... | collective-permute-start | bytes 589832 | tf_op jit(solution)/shard_map/ppermute | solution.py:286
  49.2 13.8 %collective-permute-start.13 = (bf16[128,768]{1,0:T(8,128)(2,1)S(1)}, bf16[128,768]{1,0:T(8,128)(2,1)S(1)}, u32[]{:S(2)}, u32[]{:S(2)}) collective-permute-start(bf16[128,768]{1,0:T(8,128)(2,1)S(1)} %get-tuple-element.21), channel_id=1, source_target_pairs={{0,9},{1,10},{2,11},{3,8},{4,13},{5,14},{6,15},{7,12},{8,1},{9,2},... | collective-permute-start | bytes 589832 | tf_op jit(solution)/shard_map/ppermute | solution.py:286
  56.3 14.2 %collective-permute-start.16 = (bf16[128,768]{1,0:T(8,128)(2,1)S(1)}, bf16[128,768]{1,0:T(8,128)(2,1)S(1)}, u32[]{:S(2)}, u32[]{:S(2)}) collective-permute-start(bf16[128,768]{1,0:T(8,128)(2,1)S(1)} %get-tuple-element.22), channel_id=1, source_target_pairs={{0,9},{1,10},{2,11},{3,8},{4,13},{5,14},{6,15},{7,12},{8,1},{9,2},... | collective-permute-start | bytes 589832 | tf_op jit(solution)/shard_map/ppermute | solution.py:286
  64.7 5.9 %collective-permute-start.15 = (bf16[128,768]{1,0:T(8,128)(2,1)S(1)}, bf16[128,768]{1,0:T(8,128)(2,1)S(1)}, u32[]{:S(2)}, u32[]{:S(2)}) collective-permute-start(bf16[128,768]{1,0:T(8,128)(2,1)S(1)} %shard_map.80.refs_9_), channel_id=1, source_target_pairs={{0,1},{1,2},{2,3},{4,5},{5,6},{6,7},{8,9},{9,10},{10,11},{12,13},{... | collective-permute-start | bytes 589832 | tf_op jit(solution)/shard_map/ppermute | solution.py:286
  66.1 13.3 %collective-permute-start.14 = (bf16[128,768]{1,0:T(8,128)(2,1)S(1)}, bf16[128,768]{1,0:T(8,128)(2,1)S(1)}, u32[]{:S(2)}, u32[]{:S(2)}) collective-permute-start(bf16[128,768]{1,0:T(8,128)(2,1)S(1)} %shard_map.80.refs_9_), channel_id=1, source_target_pairs={{0,9},{1,10},{2,11},{3,8},{4,13},{5,14},{6,15},{7,12},{8,1},{9,2},... | collective-permute-start | bytes 589832 | tf_op jit(solution)/shard_map/ppermute | solution.py:286
  68.2 11.1 %collective-permute-start.11 = (bf16[128,768]{1,0:T(8,128)(2,1)S(1)}, bf16[128,768]{1,0:T(8,128)(2,1)S(1)}, u32[]{:S(2)}, u32[]{:S(2)}) collective-permute-start(bf16[128,768]{1,0:T(8,128)(2,1)S(1)} %get-tuple-element.20.refs_9_), channel_id=1, source_target_pairs={{0,1},{1,2},{2,3},{3,0},{4,5},{5,6},{6,7},{7,4},{8,9},{9,10},{10,1... | collective-permute-start | bytes 589832 | tf_op jit(solution)/shard_map/ppermute | solution.py:286
  68.8 14.2 %collective-permute-start.10 = (bf16[128,768]{1,0:T(8,128)(2,1)S(1)}, bf16[128,768]{1,0:T(8,128)(2,1)S(1)}, u32[]{:S(2)}, u32[]{:S(2)}) collective-permute-start(bf16[128,768]{1,0:T(8,128)(2,1)S(1)} %get-tuple-element.19), channel_id=1, source_target_pairs={{1,0},{2,1},{3,2},{0,3},{5,4},{6,5},{7,6},{4,7},{9,8},{10,9},{11,1... | collective-permute-start | bytes 589832 | tf_op jit(solution)/shard_map/ppermute | solution.py:289
  72.2 15.8 %collective-permute-start.18 = (bf16[128,768]{1,0:T(8,128)(2,1)S(1)}, bf16[128,768]{1,0:T(8,128)(2,1)S(1)}, u32[]{:S(2)}, u32[]{:S(2)}) collective-permute-start(bf16[128,768]{1,0:T(8,128)(2,1)S(1)} %shard_map.81.refs_10_), channel_id=1, source_target_pairs={{0,8},{4,12},{8,0},{12,4},{1,9},{5,13},{9,1},{13,5},{2,10},{6,14},... | collective-permute-start | bytes 589832 | tf_op jit(solution)/shard_map/ppermute | solution.py:15
  81.0 7.0 %collective-permute-start.17 = (bf16[128,768]{1,0:T(8,128)(2,1)S(1)}, bf16[128,768]{1,0:T(8,128)(2,1)S(1)}, u32[]{:S(2)}, u32[]{:S(2)}) collective-permute-start(bf16[128,768]{1,0:T(8,128)(2,1)S(1)} %get-tuple-element.23), channel_id=1, source_target_pairs={{1,0},{2,1},{3,2},{0,3},{5,4},{6,5},{7,6},{4,7},{9,8},{10,9},{11,1... | collective-permute-start | bytes 589832 | tf_op jit(solution)/shard_map/ppermute | solution.py:289
  (3 other events, 22.7 us)
where the time goes:
time: 90.4 us; the launch traced here: 88.9 us
  waiting for transfers between devices  42.3 us (47%)
  starting transfers between devices  31.3 us (35%)
  Pallas kernels  15.1 us (17%)
    ppermute x9, waiting for transfers between devices, swapped(): lax.ppermute(x, axis, [(i, i ^ 1 << bit) for i in range(lax.axis_size(axi...  25.7 us
    ppermute x9, starting transfers between devices, swapped(): lax.ppermute(x, axis, [(i, i ^ 1 << bit) for i in range(lax.axis_size(axi...  17.8 us
    ppermute x8, waiting for transfers between devices, ahead(): return lax.ppermute(value, ('expert', 'section'), perm)  16.6 us
    ppermute x8, starting transfers between devices, ahead(): return lax.ppermute(value, ('expert', 'section'), perm)  10.4 us
    pallas_call x6, Pallas kernels, layer(): pl.pallas_call(functools.partial(layer_kernel, tick, which, TICKS - 1, do...  10 us
    pallas_call x2, Pallas kernels, cut(): pl.pallas_call(functools.partial(cut_kernel, some), out_shape=[jax.ShapeD...  3.97 us
    ppermute x2, starting transfers between devices, back(): lax.ppermute(value, 'section', [((s + 1) % legs, s) for s in range(legs)])  3.09 us
  transfers between devices with their start and end apart: 19, of which 11 were waited for; matrix products, arithmetic and copies ran while one was open for 0% of the time, Pallas kernels for 12%

commit v1 on v0

--- a/solution.py
+++ b/solution.py
@@ -107,13 +107,11 @@
 
 
 def piece_list(width):
-    third, half = width // 3, width // 6
-    return [
-        (0, 0, half, half + third),
-        (0, half, third, half + third),
-        (1, 0, third, third),
-        (1, 2 * third, third, 0),
-    ]
+    direct = width // 4
+    pieces = []
+    for m, share in ((0, width // 2), (1, (width - direct) // 2)):
+        pieces += [(m, r * (share // 3), share // 3, share) for r in range(3)]
+    return [*pieces, (1, width - direct, direct, 0)]
 
 
 def cut_kernel(some, *refs):
@@ -122,7 +120,7 @@
     group = lax.axis_index("groups")
     copies = []
     for index, ((m, first, size, share), out) in enumerate(zip(some, outs)):
-        rows = pl.ds(pl.multiple_of(group * share + first, 128), size)
+        rows = pl.ds(pl.multiple_of(group * share + first, 16), size)
         copies.append(pltpu.make_async_copy(sources[m].at[rows, :], out, sems.at[index]))
     for copy in copies:
         copy.start()
@@ -135,63 +133,49 @@
     group = lax.axis_index("groups")
     for _, first, size, share in some:
         for part in (group, 1 - group) if share else (0,):
-            rows = pl.ds(pl.multiple_of(part * share + first, 128), size)
+            rows = pl.ds(pl.multiple_of(part * share + first, 16), size)
             out_ref[rows, :] = refs.pop(0)[...]
 
 
-def from_pieces(rows, some, refs):
-    refs = list(refs)
-    group = lax.axis_index("groups")
-    total = 0.0
-    for _, first, size, share in some:
-        taken = [rows[:, first : first + size]]
-        if share:
-            other = rows[:, share + first : share + first + size]
-            taken = [jnp.where(group == 0, *pair) for pair in ((*taken, other), (other, *taken))]
-        for part in taken:
-            total += jnp.dot(part, refs.pop(0)[...], preferred_element_type=jnp.float32)
-    return total
-
-
-def layer_kernel(tick, which, last_tick, some, *refs):
+def mask_kernel(routes_ref, *refs):
+    mask_ref = refs[-1]
+    side = lax.axis_index("expert") // 2
+    for tick in range(TICKS):
+        serves = (routes_ref[tick, 0, 0] == side).astype(jnp.int32)
+        mask_ref[tick : tick + 1] = jnp.full((1, mask_ref.shape[1]), serves, jnp.int32)
+
+
+def layer_kernel(tick, which, last_tick, *refs):
     refs = list(refs)
     take = refs.pop
-    routes_ref = take(0)
-    straight_ref = take(0)
+    mask_ref, straight_ref = take(0), take(0)
     cross_ref = take(0) if tick else None
     fresh_ref = take(0) if which == 0 else None
-    gain_ref, columns_ref, up_ref, down_ref, far_up_ref = [take(0) for _ in range(5)]
-    far_down_refs = [take(0) for _ in range(1 if tick else sum(2 if p[3] else 1 for p in some))]
-    take(0)
-    y_ref = take(0)
-    side = lax.axis_index("expert") // 2
+    gain_ref, columns_ref, up_ref, down_ref, far_up_ref, far_down_ref, _ = refs[:7]
+    outs = refs[7:]
     leg = lax.axis_index("section")
     x = straight_ref[...].astype(jnp.float32)
     if tick:
         x = x + cross_ref[...].astype(jnp.float32)
         if which == 0:
-            take(0)[...] = x.astype(jnp.bfloat16)
+            outs[1][...] = x.astype(jnp.bfloat16)
             x = jnp.where(leg == 0, fresh_ref[tick - 1].astype(jnp.float32), x)
     inv_rms = lax.rsqrt(jnp.mean(x * x, axis=-1, keepdims=True) + 1e-06)
     normed = (x * inv_rms * gain_ref[...]).astype(jnp.bfloat16)
     columns = columns_ref[...].astype(jnp.float32)
-    column = jnp.where(side == 0, columns[0:1], columns[1:2])
+    column = jnp.where(lax.axis_index("expert") // 2 == 0, columns[0:1], columns[1:2])
     logit = jnp.sum(normed.astype(jnp.float32) * column, axis=-1, keepdims=True)
-    gate = jax.nn.sigmoid(logit)
     hidden = []
     for ref in (up_ref, far_up_ref):
         up = jnp.dot(normed, ref[...], preferred_element_type=jnp.float32)
         hidden.append(jnp.maximum(up, 0.0).astype(jnp.bfloat16))
     out = jnp.dot(hidden[0], down_ref[...], preferred_element_type=jnp.float32)
-    if len(far_down_refs) == 1:
-        out = out + jnp.dot(hidden[1], far_down_refs[0][...], preferred_element_type=jnp.float32)
-    else:
-        out = out + from_pieces(hidden[1], some, far_down_refs)
-    y = x + gate * out
-    y = jnp.where(routes_ref[tick, 0, 0] == side, y, 0.0).astype(jnp.bfloat16)
-    y_ref[...] = y
+    out = out + jnp.dot(hidden[1], far_down_ref[...], preferred_element_type=jnp.float32)
+    y = x + jax.nn.sigmoid(logit) * out
+    y = jnp.where(mask_ref[tick : tick + 1, :1] != 0, y, 0.0).astype(jnp.bfloat16)
+    outs[0][...] = y
     if which == 0 and tick < last_tick:
-        take(0)[...] = jnp.where(leg == lax.axis_size("section") - 1, fresh_ref[tick], y)
+        outs[-1][...] = jnp.where(leg == lax.axis_size("section") - 1, fresh_ref[tick], y)
 
 
 def gather_kernel(first_ref, second_ref, own_ref, returned_ref, out_ref):
@@ -225,9 +209,9 @@
             functools.partial(cut_kernel, some),
             out_shape=[jax.ShapeDtypeStruct((p[2], hid), jnp.bfloat16) for p in some],
             in_specs=[anywhere] * 2,
-            out_specs=[CUT_OUT] * len(some),
+            out_specs=[in_vmem] * len(some),
             scratch_shapes=[pltpu.SemaphoreType.DMA((len(some),))],
-            compiler_params=CUT_PARAMS,
+            compiler_params=pltpu.CompilerParams(vmem_limit_bytes=60 << 20),
         )(*own)
 
     sending = [*cut(pieces[:1]), *cut(pieces[1:])]
@@ -238,40 +222,42 @@
         parts[index] = [piece]
         if pieces[index][3]:
             parts[index].append(swapped(piece, "groups", 0))
-    by_matrix = [[i for i, p in enumerate(pieces) if p[0] == m] for m in (0, 1)]
 
     def join(m):
-        operands = [part for i in by_matrix[m] for part in parts[i]]
+        chosen = [i for i, p in enumerate(pieces) if p[0] == m]
+        operands = [part for i in chosen for part in parts[i]]
         return pl.pallas_call(
-            functools.partial(join_kernel, [pieces[i] for i in by_matrix[m]]),
+            functools.partial(join_kernel, [pieces[i] for i in chosen]),
             out_shape=jax.ShapeDtypeStruct((width, hid), jnp.bfloat16),
             in_specs=[in_vmem] * len(operands),
             out_specs=in_vmem,
             compiler_params=limited,
         )(*operands)
 
-    far_up = join(0)
-    far_down = join(1)
-    down_some = [pieces[i] for i in by_matrix[1]]
-    down_parts = [part for i in by_matrix[1] for part in parts[i]]
-
     columns = jnp.swapaxes(gating_columns[0], 0, 1)
+    mask = pl.pallas_call(
+        mask_kernel,
+        out_shape=jax.ShapeDtypeStruct((8, 128), jnp.int32),
+        in_specs=[pl.BlockSpec(memory_space=pltpu.SMEM)] + [in_vmem] * 5,
+        out_specs=in_vmem,
+        compiler_params=limited,
+        name="mask",
+    )(expert_choice_grid, *own, rootmean_gain, columns, arriving_microgroups)
+    weights = [rootmean_gain, columns, *own, join(0), join(1)]
     own_rows = pending_microgroups[0]
     other_rows = swapped(own_rows, "expert", 1)
     rows_shape = jax.ShapeDtypeStruct((num_rows, width), jnp.bfloat16)
 
     def layer(tick, which, inputs, after):
-        operands = [expert_choice_grid, *inputs]
+        operands = [mask, *inputs]
         if which == 0:
             operands.append(arriving_microgroups)
-        operands += [rootmean_gain, columns, *own, far_up]
-        operands += [far_down] if tick else down_parts
-        in_specs = [pl.BlockSpec(memory_space=pltpu.SMEM)] + [in_vmem] * (len(operands) - 1)
+        operands += weights
         extras = (which == 0) * ((tick > 0) + (tick + 1 < TICKS))
         return pl.pallas_call(
-            functools.partial(layer_kernel, tick, which, TICKS - 1, down_some),
+            functools.partial(layer_kernel, tick, which, TICKS - 1),
             out_shape=[rows_shape] * (1 + extras),
-            in_specs=[*in_specs, anywhere],
+            in_specs=[*[in_vmem] * len(operands), anywhere],
             out_specs=[in_vmem] * (1 + extras),
             compiler_params=pltpu.CompilerParams(vmem_limit_bytes=16 << 20),
         )(*operands, after)
@@ -317,10 +303,6 @@
     )(*outputs, done[0], returned)
 
 
-CUT_OUT = pl.BlockSpec(memory_space=pltpu.VMEM)
-CUT_PARAMS = pltpu.CompilerParams(vmem_limit_bytes=60 << 20)
-
-
 def chunk_order(tick):
     return (1, 0) if (TICKS - 1 - tick) % 2 == 0 else (0, 1)
 

time: 90.4 us -> 95.9 us (1.061)
  waiting for transfers between devices: 42.3 us -> 51.2 us
  Pallas kernels: 15.1 us -> 12.5 us
    ppermute x8, waiting for transfers between devices: 16.6 us -> 27.1 us  [ahead(): return lax.ppermute(value, ('expert', 'section'), perm)]
    ppermute x9 -> x15, waiting for transfers between devices: 25.7 us -> 23 us  [swapped(): lax.ppermute(x, axis, [(i, i ^ 1 << bit) for i in range(lax.axis_size(axi...]
    pallas_call x8 -> x9, Pallas kernels: 10.2 us -> 7.62 us  [the longest x6 6.86 us: layer(): pl.pallas_call(functools.partial(layer_kernel, tick, which, TICKS - 1), o...]
    ppermute x9 -> x15, starting transfers between devices: 17.8 us -> 19.9 us  [swapped(): lax.ppermute(x, axis, [(i, i ^ 1 << bit) for i in range(lax.axis_size(axi...]
    ppermute x2, starting transfers between devices: 3.09 us -> 1.02 us  [back(): lax.ppermute(value, 'section', [((s + 1) % legs, s) for s in range(legs)])]
    ppermute x2, waiting for transfers between devices: 0.01 us -> 1.11 us  [back(): lax.ppermute(value, 'section', [((s + 1) % legs, s) for s in range(legs)])]
  transfers between devices with their start and end apart: 19 -> 25, of which waited for: 11 -> 14; matrix products, arithmetic and copies ran while one was open for 0% -> 0% of each run, Pallas kernels for 12% -> 9%
where the time goes in v1:
time: 95.9 us; the launch traced here: 94.7 us
  waiting for transfers between devices  51.2 us (53%)
  starting transfers between devices  30.7 us (32%)
  Pallas kernels  12.5 us (13%)
    ppermute x8, waiting for transfers between devices, ahead(): return lax.ppermute(value, ('expert', 'section'), perm)  27.1 us
    ppermute x15, waiting for transfers between devices, swapped(): lax.ppermute(x, axis, [(i, i ^ 1 << bit) for i in range(lax.axis_size(axi...  23 us
    ppermute x15, starting transfers between devices, swapped(): lax.ppermute(x, axis, [(i, i ^ 1 << bit) for i in range(lax.axis_size(axi...  19.9 us
    ppermute x8, starting transfers between devices, ahead(): return lax.ppermute(value, ('expert', 'section'), perm)  9.83 us
    pallas_call x6, Pallas kernels, layer(): pl.pallas_call(functools.partial(layer_kernel, tick, which, TICKS - 1), o...  6.86 us
    pallas_call x2, Pallas kernels, cut(): pl.pallas_call(functools.partial(cut_kernel, some), out_shape=[jax.ShapeD...  4 us
  transfers between devices with their start and end apart: 25, of which 14 were waited for; matrix products, arithmetic and copies ran while one was open for 0% of the time, Pallas kernels for 9%

profile of v1, /device:TPU:0, one launch (start us, length us, event | category | flops | bytes accessed | tf_op | source)
XLA Modules:
  0.0 94.7 jit_solution(9632283900034980322)
XLA Ops:
  0.0 2.4 %shard_map.74 = (bf16[128,768]{1,0:T(8,128)(2,1)}, bf16[128,768]{1,0:T(8,128)(2,1)}, bf16[96,768]{1,0:T(8,128)(2,1)}, bf16[96,768]{1,0:T(8,128)(2,1)}, bf16[96,7...) custom-call(bf16[768,768]{1,0:T(8,128)(2,1)} %bitcast.6, bf16[768,768]{1,0:T(8,128)(2,1)} %bitcast.15), custom_call_target="tpu_custom_call" | custom-call | tf_op jit(solution)/shard_map/pallas_call | solution.py:208
  2.5 3.1 %collective-permute-start.6 = (bf16[96,768]{1,0:T(8,128)(2,1)}, bf16[96,768]{1,0:T(8,128)(2,1)S(1)}, u32[]{:S(2)}, u32[]{:S(2)}) collective-permute-start(bf16[96,768]{1,0:T(8,128)(2,1)} %get-tuple-element.20), channel_id=1, source_target_pairs={{0,4},{4,0},{8,12},{12,8},{1,5},{5,1},{9,13},{13,9},{2,6},{6,2},{1... | collective-permute-start | bytes 442376 | tf_op jit(solution)/shard_map/ppermute | solution.py:15
  5.6 1.6 %shard_map.73 = bf16[128,768]{1,0:T(8,128)(2,1)} custom-call(bf16[768,768]{1,0:T(8,128)(2,1)} %bitcast.7, bf16[768,768]{1,0:T(8,128)(2,1)} %bitcast.16), custom_call_target="tpu_custom_call" | custom-call | tf_op jit(solution)/shard_map/pallas_call | solution.py:208
  7.5 1.9 %collective-permute-start.8 = (bf16[96,768]{1,0:T(8,128)(2,1)}, bf16[96,768]{1,0:T(8,128)(2,1)S(1)}, u32[]{:S(2)}, u32[]{:S(2)}) collective-permute-start(bf16[96,768]{1,0:T(8,128)(2,1)} %get-tuple-element.21), channel_id=1, source_target_pairs={{0,4},{4,0},{8,12},{12,8},{1,5},{5,1},{9,13},{13,9},{2,6},{6,2},{1... | collective-permute-start | bytes 442376 | tf_op jit(solution)/shard_map/ppermute | solution.py:15
  9.5 1.9 %collective-permute-start.10 = (bf16[96,768]{1,0:T(8,128)(2,1)}, bf16[96,768]{1,0:T(8,128)(2,1)S(1)}, u32[]{:S(2)}, u32[]{:S(2)}) collective-permute-start(bf16[96,768]{1,0:T(8,128)(2,1)} %get-tuple-element.22), channel_id=1, source_target_pairs={{0,4},{4,0},{8,12},{12,8},{1,5},{5,1},{9,13},{13,9},{2,6},{6,2},{1... | collective-permute-start | bytes 442376 | tf_op jit(solution)/shard_map/ppermute | solution.py:15
  12.5 5.9 %collective-permute-done.8.refs_2_ = bf16[96,768]{1,0:T(8,128)(2,1)S(1)} collective-permute-done((bf16[96,768]{1,0:T(8,128)(2,1)}, bf16[96,768]{1,0:T(8,128)(2,1)S(1)}, u32[]{:S(2)}, u32[]{:S(2)}) %collective-permute-start.8) | collective-permute-done | bytes 147488 | tf_op jit(solution)/shard_map/ppermute | solution.py:15
  18.4 1.5 %collective-permute-start.7 = (bf16[96,768]{1,0:T(8,128)(2,1)S(1)}, bf16[96,768]{1,0:T(8,128)(2,1)S(1)}, u32[]{:S(2)}, u32[]{:S(2)}) collective-permute-start(bf16[96,768]{1,0:T(8,128)(2,1)S(1)} %collective-permute-done.6.refs_0_), channel_id=1, source_target_pairs={{0,16},{16,0},{1,17},{17,1},{2,18},{18,2},{3,19},{19,3},{4,20},{20... | collective-permute-start | bytes 442376 | tf_op jit(solution)/shard_map/ppermute | solution.py:15
  19.9 5.9 %collective-permute-done.10.refs_4_ = bf16[96,768]{1,0:T(8,128)(2,1)S(1)} collective-permute-done((bf16[96,768]{1,0:T(8,128)(2,1)}, bf16[96,768]{1,0:T(8,128)(2,1)S(1)}, u32[]{:S(2)}, u32[]{:S(2)}) %collective-permute-start.10) | collective-permute-done | bytes 147488 | tf_op jit(solution)/shard_map/ppermute | solution.py:15
  25.8 1.5 %collective-permute-start.9 = (bf16[96,768]{1,0:T(8,128)(2,1)S(1)}, bf16[96,768]{1,0:T(8,128)(2,1)S(1)}, u32[]{:S(2)}, u32[]{:S(2)}) collective-permute-start(bf16[96,768]{1,0:T(8,128)(2,1)S(1)} %collective-permute-done.8.refs_2_), channel_id=1, source_target_pairs={{0,16},{16,0},{1,17},{17,1},{2,18},{18,2},{3,19},{19,3},{4,20},{20... | collective-permute-start | bytes 442376 | tf_op jit(solution)/shard_map/ppermute | solution.py:15
  27.8 1.5 %collective-permute-start.12 = (bf16[192,768]{1,0:T(8,128)(2,1)}, bf16[192,768]{1,0:T(8,128)(2,1)S(1)}, u32[]{:S(2)}, u32[]{:S(2)}) collective-permute-start(bf16[192,768]{1,0:T(8,128)(2,1)} %get-tuple-element.23), channel_id=1, source_target_pairs={{0,4},{4,0},{8,12},{12,8},{1,5},{5,1},{9,13},{13,9},{2,6},{6,2},{1... | collective-permute-start | bytes 884744 | tf_op jit(solution)/shard_map/ppermute | solution.py:15
  29.6 1.8 %collective-permute-start.1 = (bf16[128,768]{1,0:T(8,128)(2,1)S(1)}, bf16[128,768]{1,0:T(8,128)(2,1)S(1)}, u32[]{:S(2)}, u32[]{:S(2)}) collective-permute-start(bf16[128,768]{1,0:T(8,128)(2,1)S(1)} %collective-permute-done.refs_0_), channel_id=1, source_target_pairs={{0,16},{16,0},{1,17},{17,1},{2,18},{18,2},{3,19},{19,3},{4,20},{20... | collective-permute-start | bytes 589832 | tf_op jit(solution)/shard_map/ppermute | solution.py:15
  31.8 1.5 %collective-permute-start.5 = (bf16[128,768]{1,0:T(8,128)(2,1)S(1)}, bf16[128,768]{1,0:T(8,128)(2,1)S(1)}, u32[]{:S(2)}, u32[]{:S(2)}) collective-permute-start(bf16[128,768]{1,0:T(8,128)(2,1)S(1)} %collective-permute-done.4.refs_4_), channel_id=1, source_target_pairs={{0,16},{16,0},{1,17},{17,1},{2,18},{18,2},{3,19},{19,3},{4,20},{20... | collective-permute-start | bytes 589832 | tf_op jit(solution)/shard_map/ppermute | solution.py:15
  33.4 1.6 %collective-permute-done.11.refs_5_ = bf16[96,768]{1,0:T(8,128)(2,1)S(1)} collective-permute-done((bf16[96,768]{1,0:T(8,128)(2,1)S(1)}, bf16[96,768]{1,0:T(8,128)(2,1)S(1)}, u32[]{:S(2)}, u32[]{:S(2)}) %collective-permute-start.11) | collective-permute-done | bytes 147488 | tf_op jit(solution)/shard_map/ppermute | solution.py:15
  35.0 2.4 %collective-permute-start.13 = (bf16[128,768]{1,0:T(8,128)(2,1)S(1)}, bf16[128,768]{1,0:T(8,128)(2,1)S(1)}, u32[]{:S(2)}, u32[]{:S(2)}) collective-permute-start(bf16[128,768]{1,0:T(8,128)(2,1)S(1)} %bitcast.24), channel_id=1, source_target_pairs={{0,8},{4,12},{8,0},{12,4},{1,9},{5,13},{9,1},{13,5},{2,10},{6,14},... | collective-permute-start | bytes 589832 | tf_op jit(solution)/shard_map/ppermute | solution.py:15
  39.2 3.8 %collective-permute-done.3.refs_3_ = bf16[128,768]{1,0:T(8,128)(2,1)S(1)} collective-permute-done((bf16[128,768]{1,0:T(8,128)(2,1)S(1)}, bf16[128,768]{1,0:T(8,128)(2,1)S(1)}, u32[]{:S(2)}, u32[]{:S(2)}) %collective-permute-start.3) | collective-permute-done | bytes 196640 | tf_op jit(solution)/shard_map/ppermute | solution.py:15
  43.1 2.1 %collective-permute-done.5.refs_5_ = bf16[128,768]{1,0:T(8,128)(2,1)S(1)} collective-permute-done((bf16[128,768]{1,0:T(8,128)(2,1)S(1)}, bf16[128,768]{1,0:T(8,128)(2,1)S(1)}, u32[]{:S(2)}, u32[]{:S(2)}) %collective-permute-start.5) | collective-permute-done | bytes 196640 | tf_op jit(solution)/shard_map/ppermute | solution.py:15
  47.7 3.6 %collective-permute-start.14 = (bf16[128,768]{1,0:T(8,128)(2,1)S(1)}, bf16[128,768]{1,0:T(8,128)(2,1)S(1)}, u32[]{:S(2)}, u32[]{:S(2)}) collective-permute-start(bf16[128,768]{1,0:T(8,128)(2,1)S(1)} %get-tuple-element.24.refs_10_), channel_id=1, source_target_pairs={{0,1},{1,2},{2,3},{3,0},{4,5},{5,6},{6,7},{7,4},{8,9},{9,10},{10,1... | collective-permute-start | bytes 589832 | tf_op jit(solution)/shard_map/ppermute | solution.py:272
  51.3 1.9 %collective-permute-start.18 = (bf16[128,768]{1,0:T(8,128)(2,1)S(1)}, bf16[128,768]{1,0:T(8,128)(2,1)S(1)}, u32[]{:S(2)}, u32[]{:S(2)}) collective-permute-start(bf16[128,768]{1,0:T(8,128)(2,1)S(1)} %shard_map.77.refs_9_), channel_id=1, source_target_pairs={{0,1},{1,2},{2,3},{4,5},{5,6},{6,7},{8,9},{9,10},{10,11},{12,13},{... | collective-permute-start | bytes 589832 | tf_op jit(solution)/shard_map/ppermute | solution.py:272
  53.8 9.8 %collective-permute-done.15.refs_2_ = bf16[128,768]{1,0:T(8,128)(2,1)S(1)} collective-permute-done((bf16[128,768]{1,0:T(8,128)(2,1)S(1)}, bf16[128,768]{1,0:T(8,128)(2,1)S(1)}, u32[]{:S(2)}, u32[]{:S(2)}) %collective-permute-start.15) | collective-permute-done | bytes 196640 | tf_op jit(solution)/shard_map/ppermute | solution.py:272
  64.9 7.2 %collective-permute-done.19.refs_2_ = bf16[128,768]{1,0:T(8,128)(2,1)S(1)} collective-permute-done((bf16[128,768]{1,0:T(8,128)(2,1)S(1)}, bf16[128,768]{1,0:T(8,128)(2,1)S(1)}, u32[]{:S(2)}, u32[]{:S(2)}) %collective-permute-start.19) | collective-permute-done | bytes 196640 | tf_op jit(solution)/shard_map/ppermute | solution.py:272
  75.4 1.3 %collective-permute-start.17 = (bf16[128,768]{1,0:T(8,128)(2,1)S(1)}, bf16[128,768]{1,0:T(8,128)(2,1)S(1)}, u32[]{:S(2)}, u32[]{:S(2)}) collective-permute-start(bf16[128,768]{1,0:T(8,128)(2,1)S(1)} %get-tuple-element.26.refs_9_), channel_id=1, source_target_pairs={{0,1},{1,2},{2,3},{3,0},{4,5},{5,6},{6,7},{7,4},{8,9},{9,10},{10,1... | collective-permute-start | bytes 589832 | tf_op jit(solution)/shard_map/ppermute | solution.py:272
  77.1 3.3 %collective-permute-done.22.refs_2_ = bf16[128,768]{1,0:T(8,128)(2,1)S(1)} collective-permute-done((bf16[128,768]{1,0:T(8,128)(2,1)S(1)}, bf16[128,768]{1,0:T(8,128)(2,1)S(1)}, u32[]{:S(2)}, u32[]{:S(2)}) %collective-permute-start.22) | collective-permute-done | bytes 196640 | tf_op jit(solution)/shard_map/ppermute | solution.py:272
  82.1 6.8 %collective-permute-done.20.refs_2_ = bf16[128,768]{1,0:T(8,128)(2,1)S(1)} collective-permute-done((bf16[128,768]{1,0:T(8,128)(2,1)S(1)}, bf16[128,768]{1,0:T(8,128)(2,1)S(1)}, u32[]{:S(2)}, u32[]{:S(2)}) %collective-permute-start.20) | collective-permute-done | bytes 196640 | tf_op jit(solution)/shard_map/ppermute | solution.py:272
  90.7 2.1 %collective-permute-done.24.returned_ref = bf16[128,768]{1,0:T(8,128)(2,1)S(1)} collective-permute-done((bf16[128,768]{1,0:T(8,128)(2,1)S(1)}, bf16[128,768]{1,0:T(8,128)(2,1)S(1)}, u32[]{:S(2)}, u32[]{:S(2)}) %collective-permute-start.24) | collective-permute-done | bytes 196640 | tf_op jit(solution)/shard_map/ppermute | solution.py:15
  (52 shorter events, 18.1 us)
Async XLA Ops:
  2.5 8.9 %collective-permute-start.6 = (bf16[96,768]{1,0:T(8,128)(2,1)}, bf16[96,768]{1,0:T(8,128)(2,1)S(1)}, u32[]{:S(2)}, u32[]{:S(2)}) collective-permute-start(bf16[96,768]{1,0:T(8,128)(2,1)} %get-tuple-element.20), channel_id=1, source_target_pairs={{0,4},{4,0},{8,12},{12,8},{1,5},{5,1},{9,13},{13,9},{2,6},{6,2},{1... | collective-permute-start | bytes 442376 | tf_op jit(solution)/shard_map/ppermute | solution.py:15
  7.2 20.1 %collective-permute-start = (bf16[128,768]{1,0:T(8,128)(2,1)}, bf16[128,768]{1,0:T(8,128)(2,1)S(1)}, u32[]{:S(2)}, u32[]{:S(2)}) collective-permute-start(bf16[128,768]{1,0:T(8,128)(2,1)} %shard_map.73), channel_id=1, source_target_pairs={{0,4},{4,0},{8,12},{12,8},{1,5},{5,1},{9,13},{13,9},{2,6},{6,2},{1... | collective-permute-start | bytes 589832 | tf_op jit(solution)/shard_map/ppermute | solution.py:15
  7.5 11.0 %collective-permute-start.8 = (bf16[96,768]{1,0:T(8,128)(2,1)}, bf16[96,768]{1,0:T(8,128)(2,1)S(1)}, u32[]{:S(2)}, u32[]{:S(2)}) collective-permute-start(bf16[96,768]{1,0:T(8,128)(2,1)} %get-tuple-element.21), channel_id=1, source_target_pairs={{0,4},{4,0},{8,12},{12,8},{1,5},{5,1},{9,13},{13,9},{2,6},{6,2},{1... | collective-permute-start | bytes 442376 | tf_op jit(solution)/shard_map/ppermute | solution.py:15
  9.3 18.5 %collective-permute-start.2 = (bf16[128,768]{1,0:T(8,128)(2,1)}, bf16[128,768]{1,0:T(8,128)(2,1)S(1)}, u32[]{:S(2)}, u32[]{:S(2)}) collective-permute-start(bf16[128,768]{1,0:T(8,128)(2,1)} %get-tuple-element.18), channel_id=1, source_target_pairs={{0,4},{4,0},{8,12},{12,8},{1,5},{5,1},{9,13},{13,9},{2,6},{6,2},{1... | collective-permute-start | bytes 589832 | tf_op jit(solution)/shard_map/ppermute | solution.py:15
  9.5 16.3 %collective-permute-start.10 = (bf16[96,768]{1,0:T(8,128)(2,1)}, bf16[96,768]{1,0:T(8,128)(2,1)S(1)}, u32[]{:S(2)}, u32[]{:S(2)}) collective-permute-start(bf16[96,768]{1,0:T(8,128)(2,1)} %get-tuple-element.22), channel_id=1, source_target_pairs={{0,4},{4,0},{8,12},{12,8},{1,5},{5,1},{9,13},{13,9},{2,6},{6,2},{1... | collective-permute-start | bytes 442376 | tf_op jit(solution)/shard_map/ppermute | solution.py:15
  11.3 18.2 %collective-permute-start.4 = (bf16[128,768]{1,0:T(8,128)(2,1)}, bf16[128,768]{1,0:T(8,128)(2,1)S(1)}, u32[]{:S(2)}, u32[]{:S(2)}) collective-permute-start(bf16[128,768]{1,0:T(8,128)(2,1)} %get-tuple-element.19), channel_id=1, source_target_pairs={{0,4},{4,0},{8,12},{12,8},{1,5},{5,1},{9,13},{13,9},{2,6},{6,2},{1... | collective-permute-start | bytes 589832 | tf_op jit(solution)/shard_map/ppermute | solution.py:15
  18.4 12.9 %collective-permute-start.7 = (bf16[96,768]{1,0:T(8,128)(2,1)S(1)}, bf16[96,768]{1,0:T(8,128)(2,1)S(1)}, u32[]{:S(2)}, u32[]{:S(2)}) collective-permute-start(bf16[96,768]{1,0:T(8,128)(2,1)S(1)} %collective-permute-done.6.refs_0_), channel_id=1, source_target_pairs={{0,16},{16,0},{1,17},{17,1},{2,18},{18,2},{3,19},{19,3},{4,20},{20... | collective-permute-start | bytes 442376 | tf_op jit(solution)/shard_map/ppermute | solution.py:15
  25.8 6.0 %collective-permute-start.9 = (bf16[96,768]{1,0:T(8,128)(2,1)S(1)}, bf16[96,768]{1,0:T(8,128)(2,1)S(1)}, u32[]{:S(2)}, u32[]{:S(2)}) collective-permute-start(bf16[96,768]{1,0:T(8,128)(2,1)S(1)} %collective-permute-done.8.refs_2_), channel_id=1, source_target_pairs={{0,16},{16,0},{1,17},{17,1},{2,18},{18,2},{3,19},{19,3},{4,20},{20... | collective-permute-start | bytes 442376 | tf_op jit(solution)/shard_map/ppermute | solution.py:15
  27.3 7.7 %collective-permute-start.11 = (bf16[96,768]{1,0:T(8,128)(2,1)S(1)}, bf16[96,768]{1,0:T(8,128)(2,1)S(1)}, u32[]{:S(2)}, u32[]{:S(2)}) collective-permute-start(bf16[96,768]{1,0:T(8,128)(2,1)S(1)} %collective-permute-done.10.refs_4_), channel_id=1, source_target_pairs={{0,16},{16,0},{1,17},{17,1},{2,18},{18,2},{3,19},{19,3},{4,20},{20... | collective-permute-start | bytes 442376 | tf_op jit(solution)/shard_map/ppermute | solution.py:15
  27.8 10.2 %collective-permute-start.12 = (bf16[192,768]{1,0:T(8,128)(2,1)}, bf16[192,768]{1,0:T(8,128)(2,1)S(1)}, u32[]{:S(2)}, u32[]{:S(2)}) collective-permute-start(bf16[192,768]{1,0:T(8,128)(2,1)} %get-tuple-element.23), channel_id=1, source_target_pairs={{0,4},{4,0},{8,12},{12,8},{1,5},{5,1},{9,13},{13,9},{2,6},{6,2},{1... | collective-permute-start | bytes 884744 | tf_op jit(solution)/shard_map/ppermute | solution.py:15
  29.6 9.6 %collective-permute-start.1 = (bf16[128,768]{1,0:T(8,128)(2,1)S(1)}, bf16[128,768]{1,0:T(8,128)(2,1)S(1)}, u32[]{:S(2)}, u32[]{:S(2)}) collective-permute-start(bf16[128,768]{1,0:T(8,128)(2,1)S(1)} %collective-permute-done.refs_0_), channel_id=1, source_target_pairs={{0,16},{16,0},{1,17},{17,1},{2,18},{18,2},{3,19},{19,3},{4,20},{20... | collective-permute-start | bytes 589832 | tf_op jit(solution)/shard_map/ppermute | solution.py:15
  31.4 11.7 %collective-permute-start.3 = (bf16[128,768]{1,0:T(8,128)(2,1)S(1)}, bf16[128,768]{1,0:T(8,128)(2,1)S(1)}, u32[]{:S(2)}, u32[]{:S(2)}) collective-permute-start(bf16[128,768]{1,0:T(8,128)(2,1)S(1)} %collective-permute-done.2.refs_2_), channel_id=1, source_target_pairs={{0,16},{16,0},{1,17},{17,1},{2,18},{18,2},{3,19},{19,3},{4,20},{20... | collective-permute-start | bytes 589832 | tf_op jit(solution)/shard_map/ppermute | solution.py:15
  31.8 13.3 %collective-permute-start.5 = (bf16[128,768]{1,0:T(8,128)(2,1)S(1)}, bf16[128,768]{1,0:T(8,128)(2,1)S(1)}, u32[]{:S(2)}, u32[]{:S(2)}) collective-permute-start(bf16[128,768]{1,0:T(8,128)(2,1)S(1)} %collective-permute-done.4.refs_4_), channel_id=1, source_target_pairs={{0,16},{16,0},{1,17},{17,1},{2,18},{18,2},{3,19},{19,3},{4,20},{20... | collective-permute-start | bytes 589832 | tf_op jit(solution)/shard_map/ppermute | solution.py:15
  35.0 10.3 %collective-permute-start.13 = (bf16[128,768]{1,0:T(8,128)(2,1)S(1)}, bf16[128,768]{1,0:T(8,128)(2,1)S(1)}, u32[]{:S(2)}, u32[]{:S(2)}) collective-permute-start(bf16[128,768]{1,0:T(8,128)(2,1)S(1)} %bitcast.24), channel_id=1, source_target_pairs={{0,8},{4,12},{8,0},{12,4},{1,9},{5,13},{9,1},{13,5},{2,10},{6,14},... | collective-permute-start | bytes 589832 | tf_op jit(solution)/shard_map/ppermute | solution.py:15
  46.4 17.2 %collective-permute-start.15 = (bf16[128,768]{1,0:T(8,128)(2,1)S(1)}, bf16[128,768]{1,0:T(8,128)(2,1)S(1)}, u32[]{:S(2)}, u32[]{:S(2)}) collective-permute-start(bf16[128,768]{1,0:T(8,128)(2,1)S(1)} %shard_map.77.refs_9_), channel_id=1, source_target_pairs={{0,9},{1,10},{2,11},{3,8},{4,13},{5,14},{6,15},{7,12},{8,1},{9,2},... | collective-permute-start | bytes 589832 | tf_op jit(solution)/shard_map/ppermute | solution.py:272
  47.7 16.0 %collective-permute-start.14 = (bf16[128,768]{1,0:T(8,128)(2,1)S(1)}, bf16[128,768]{1,0:T(8,128)(2,1)S(1)}, u32[]{:S(2)}, u32[]{:S(2)}) collective-permute-start(bf16[128,768]{1,0:T(8,128)(2,1)S(1)} %get-tuple-element.24.refs_10_), channel_id=1, source_target_pairs={{0,1},{1,2},{2,3},{3,0},{4,5},{5,6},{6,7},{7,4},{8,9},{9,10},{10,1... | collective-permute-start | bytes 589832 | tf_op jit(solution)/shard_map/ppermute | solution.py:272
  51.3 13.6 %collective-permute-start.18 = (bf16[128,768]{1,0:T(8,128)(2,1)S(1)}, bf16[128,768]{1,0:T(8,128)(2,1)S(1)}, u32[]{:S(2)}, u32[]{:S(2)}) collective-permute-start(bf16[128,768]{1,0:T(8,128)(2,1)S(1)} %shard_map.77.refs_9_), channel_id=1, source_target_pairs={{0,1},{1,2},{2,3},{4,5},{5,6},{6,7},{8,9},{9,10},{10,11},{12,13},{... | collective-permute-start | bytes 589832 | tf_op jit(solution)/shard_map/ppermute | solution.py:272
  53.2 18.8 %collective-permute-start.19 = (bf16[128,768]{1,0:T(8,128)(2,1)S(1)}, bf16[128,768]{1,0:T(8,128)(2,1)S(1)}, u32[]{:S(2)}, u32[]{:S(2)}) collective-permute-start(bf16[128,768]{1,0:T(8,128)(2,1)S(1)} %get-tuple-element.27), channel_id=1, source_target_pairs={{0,9},{1,10},{2,11},{3,8},{4,13},{5,14},{6,15},{7,12},{8,1},{9,2},... | collective-permute-start | bytes 589832 | tf_op jit(solution)/shard_map/ppermute | solution.py:272
  64.8 15.7 %collective-permute-start.22 = (bf16[128,768]{1,0:T(8,128)(2,1)S(1)}, bf16[128,768]{1,0:T(8,128)(2,1)S(1)}, u32[]{:S(2)}, u32[]{:S(2)}) collective-permute-start(bf16[128,768]{1,0:T(8,128)(2,1)S(1)} %get-tuple-element.28), channel_id=1, source_target_pairs={{0,9},{1,10},{2,11},{3,8},{4,13},{5,14},{6,15},{7,12},{8,1},{9,2},... | collective-permute-start | bytes 589832 | tf_op jit(solution)/shard_map/ppermute | solution.py:272
  73.2 7.3 %collective-permute-start.21 = (bf16[128,768]{1,0:T(8,128)(2,1)S(1)}, bf16[128,768]{1,0:T(8,128)(2,1)S(1)}, u32[]{:S(2)}, u32[]{:S(2)}) collective-permute-start(bf16[128,768]{1,0:T(8,128)(2,1)S(1)} %shard_map.80.refs_9_), channel_id=1, source_target_pairs={{0,1},{1,2},{2,3},{4,5},{5,6},{6,7},{8,9},{9,10},{10,11},{12,13},{... | collective-permute-start | bytes 589832 | tf_op jit(solution)/shard_map/ppermute | solution.py:272
  74.5 14.4 %collective-permute-start.20 = (bf16[128,768]{1,0:T(8,128)(2,1)S(1)}, bf16[128,768]{1,0:T(8,128)(2,1)S(1)}, u32[]{:S(2)}, u32[]{:S(2)}) collective-permute-start(bf16[128,768]{1,0:T(8,128)(2,1)S(1)} %shard_map.80.refs_9_), channel_id=1, source_target_pairs={{0,9},{1,10},{2,11},{3,8},{4,13},{5,14},{6,15},{7,12},{8,1},{9,2},... | collective-permute-start | bytes 589832 | tf_op jit(solution)/shard_map/ppermute | solution.py:272
  75.4 13.5 %collective-permute-start.17 = (bf16[128,768]{1,0:T(8,128)(2,1)S(1)}, bf16[128,768]{1,0:T(8,128)(2,1)S(1)}, u32[]{:S(2)}, u32[]{:S(2)}) collective-permute-start(bf16[128,768]{1,0:T(8,128)(2,1)S(1)} %get-tuple-element.26.refs_9_), channel_id=1, source_target_pairs={{0,1},{1,2},{2,3},{3,0},{4,5},{5,6},{6,7},{7,4},{8,9},{9,10},{10,1... | collective-permute-start | bytes 589832 | tf_op jit(solution)/shard_map/ppermute | solution.py:272
  76.7 14.0 %collective-permute-start.16 = (bf16[128,768]{1,0:T(8,128)(2,1)S(1)}, bf16[128,768]{1,0:T(8,128)(2,1)S(1)}, u32[]{:S(2)}, u32[]{:S(2)}) collective-permute-start(bf16[128,768]{1,0:T(8,128)(2,1)S(1)} %get-tuple-element.25), channel_id=1, source_target_pairs={{1,0},{2,1},{3,2},{0,3},{5,4},{6,5},{7,6},{4,7},{9,8},{10,9},{11,1... | collective-permute-start | bytes 589832 | tf_op jit(solution)/shard_map/ppermute | solution.py:275
  81.6 11.1 %collective-permute-start.24 = (bf16[128,768]{1,0:T(8,128)(2,1)S(1)}, bf16[128,768]{1,0:T(8,128)(2,1)S(1)}, u32[]{:S(2)}, u32[]{:S(2)}) collective-permute-start(bf16[128,768]{1,0:T(8,128)(2,1)S(1)} %shard_map.81.refs_10_), channel_id=1, source_target_pairs={{0,8},{4,12},{8,0},{12,4},{1,9},{5,13},{9,1},{13,5},{2,10},{6,14},... | collective-permute-start | bytes 589832 | tf_op jit(solution)/shard_map/ppermute | solution.py:15
  (8 other events, 248.5 us)

commit v2 on v1

--- a/solution.py
+++ b/solution.py
@@ -107,7 +107,7 @@
 
 
 def piece_list(width):
-    direct = width // 4
+    direct = width // 8
     pieces = []
     for m, share in ((0, width // 2), (1, (width - direct) // 2)):
         pieces += [(m, r * (share // 3), share // 3, share) for r in range(3)]
@@ -149,13 +149,13 @@
     refs = list(refs)
     take = refs.pop
     mask_ref, straight_ref = take(0), take(0)
-    cross_ref = take(0) if tick else None
+    cross_ref = take(0) if tick or which else None
     fresh_ref = take(0) if which == 0 else None
     gain_ref, columns_ref, up_ref, down_ref, far_up_ref, far_down_ref, _ = refs[:7]
     outs = refs[7:]
     leg = lax.axis_index("section")
     x = straight_ref[...].astype(jnp.float32)
-    if tick:
+    if tick or which:
         x = x + cross_ref[...].astype(jnp.float32)
         if which == 0:
             outs[1][...] = x.astype(jnp.bfloat16)
@@ -207,11 +207,11 @@
     def cut(some):
         return pl.pallas_call(
             functools.partial(cut_kernel, some),
-            out_shape=[jax.ShapeDtypeStruct((p[2], hid), jnp.bfloat16) for p in some],
+            out_shape=[pltpu.VMEM((p[2], hid), jnp.bfloat16) for p in some],
             in_specs=[anywhere] * 2,
             out_specs=[in_vmem] * len(some),
             scratch_shapes=[pltpu.SemaphoreType.DMA((len(some),))],
-            compiler_params=pltpu.CompilerParams(vmem_limit_bytes=60 << 20),
+            compiler_params=pltpu.CompilerParams(vmem_limit_bytes=58 << 20),
         )(*own)
 
     sending = [*cut(pieces[:1]), *cut(pieces[1:])]
@@ -245,7 +245,9 @@
     )(expert_choice_grid, *own, rootmean_gain, columns, arriving_microgroups)
     weights = [rootmean_gain, columns, *own, join(0), join(1)]
     own_rows = pending_microgroups[0]
-    other_rows = swapped(own_rows, "expert", 1)
+    other_rows = []
+    for senders in ((0, places - 1), range(1, places - 1)):
+        other_rows.append(lax.ppermute(own_rows, "expert", [(e, e ^ 2) for e in senders]))
     rows_shape = jax.ShapeDtypeStruct((num_rows, width), jnp.bfloat16)
 
     def layer(tick, which, inputs, after):
@@ -274,7 +276,7 @@
     def back(value):
         return lax.ppermute(value, "section", [((s + 1) % legs, s) for s in range(legs)])
 
-    current = {0: (own_rows,), 1: (other_rows,)}
+    current = {0: (own_rows,), 1: other_rows}
     outputs = []
     after = own_rows
     for tick in range(TICKS):

time: 95.9 us -> 95.8 us (level)
  starting transfers between devices: 30.7 us -> 36.7 us
  waiting for transfers between devices: 51.2 us -> 47.5 us
  Pallas kernels: 12.5 us -> 10.8 us
    ppermute x0 -> x2, starting transfers between devices: none -> 6.72 us  [pairs_per_device(): lax.ppermute(own_rows, 'expert', [(e, e ^ 2) for e in senders])]
    ppermute x8, waiting for transfers between devices: 27.1 us -> 21.8 us  [ahead(): return lax.ppermute(value, ('expert', 'section'), perm)]
    ppermute x15 -> x14, waiting for transfers between devices: 23 us -> 25.7 us  [swapped(): lax.ppermute(x, axis, [(i, i ^ 1 << bit) for i in range(lax.axis_size(axi...]
    ppermute x15 -> x14, starting transfers between devices: 19.9 us -> 17.3 us  [swapped(): lax.ppermute(x, axis, [(i, i ^ 1 << bit) for i in range(lax.axis_size(axi...]
    pallas_call x2, Pallas kernels: 4 us -> 2.32 us  [cut(): pl.pallas_call(functools.partial(cut_kernel, some), out_shape=[pltpu.VMEM...]
    ppermute x2, waiting for transfers between devices: 1.11 us -> 0.01 us  [back(): lax.ppermute(value, 'section', [((s + 1) % legs, s) for s in range(legs)])]
    ppermute x8, starting transfers between devices: 9.83 us -> 10.9 us  [ahead(): return lax.ppermute(value, ('expert', 'section'), perm)]
  transfers between devices with their start and end apart: 25 -> 26, of which waited for: 14 -> 12; matrix products, arithmetic and copies ran while one was open for 0% -> 0% of each run, Pallas kernels for 9% -> 8%
where the time goes in v2:
time: 95.8 us; the launch traced here: 95.3 us
  waiting for transfers between devices  47.5 us (50%)
  starting transfers between devices  36.7 us (38%)
  Pallas kernels  10.8 us (11%)
    ppermute x14, waiting for transfers between devices, swapped(): lax.ppermute(x, axis, [(i, i ^ 1 << bit) for i in range(lax.axis_size(axi...  25.7 us
    ppermute x8, waiting for transfers between devices, ahead(): return lax.ppermute(value, ('expert', 'section'), perm)  21.8 us
    ppermute x14, starting transfers between devices, swapped(): lax.ppermute(x, axis, [(i, i ^ 1 << bit) for i in range(lax.axis_size(axi...  17.3 us
    ppermute x8, starting transfers between devices, ahead(): return lax.ppermute(value, ('expert', 'section'), perm)  10.9 us
    pallas_call x6, Pallas kernels, layer(): pl.pallas_call(functools.partial(layer_kernel, tick, which, TICKS - 1), o...  6.83 us
    ppermute x2, starting transfers between devices, pairs_per_device(): lax.ppermute(own_rows, 'expert', [(e, e ^ 2) for e in senders])  6.72 us
    pallas_call x2, Pallas kernels, cut(): pl.pallas_call(functools.partial(cut_kernel, some), out_shape=[pltpu.VMEM...  2.32 us
  transfers between devices with their start and end apart: 26, of which 12 were waited for; matrix products, arithmetic and copies ran while one was open for 0% of the time, Pallas kernels for 8%

profile of v2, /device:TPU:0, one launch (start us, length us, event | category | flops | bytes accessed | tf_op | source)
XLA Modules:
  0.0 95.3 jit_solution(14295686858607297155)
XLA Ops:
  1.5 3.1 %collective-permute-start.6 = (bf16[112,768]{1,0:T(8,128)(2,1)S(1)}, bf16[112,768]{1,0:T(8,128)(2,1)S(1)}, u32[]{:S(2)}, u32[]{:S(2)}) collective-permute-start(bf16[112,768]{1,0:T(8,128)(2,1)S(1)} %get-tuple-element.20), channel_id=1, source_target_pairs={{0,4},{4,0},{8,12},{12,8},{1,5},{5,1},{9,13},{13,9},{2,6},{6,2},{1... | collective-permute-start | bytes 516104 | tf_op jit(solution)/shard_map/ppermute | solution.py:15
  5.8 1.8 %collective-permute-start.12 = (bf16[96,768]{1,0:T(8,128)(2,1)S(1)}, bf16[96,768]{1,0:T(8,128)(2,1)S(1)}, u32[]{:S(2)}, u32[]{:S(2)}) collective-permute-start(bf16[96,768]{1,0:T(8,128)(2,1)S(1)} %get-tuple-element.23), channel_id=1, source_target_pairs={{0,4},{4,0},{8,12},{12,8},{1,5},{5,1},{9,13},{13,9},{2,6},{6,2},{1... | collective-permute-start | bytes 442376 | tf_op jit(solution)/shard_map/ppermute | solution.py:15
  7.8 1.8 %collective-permute-start.10 = (bf16[112,768]{1,0:T(8,128)(2,1)S(1)}, bf16[112,768]{1,0:T(8,128)(2,1)S(1)}, u32[]{:S(2)}, u32[]{:S(2)}) collective-permute-start(bf16[112,768]{1,0:T(8,128)(2,1)S(1)} %get-tuple-element.22), channel_id=1, source_target_pairs={{0,4},{4,0},{8,12},{12,8},{1,5},{5,1},{9,13},{13,9},{2,6},{6,2},{1... | collective-permute-start | bytes 516104 | tf_op jit(solution)/shard_map/ppermute | solution.py:15
  9.6 7.5 %collective-permute-done.12.refs_6_ = bf16[96,768]{1,0:T(8,128)(2,1)S(1)} collective-permute-done((bf16[96,768]{1,0:T(8,128)(2,1)S(1)}, bf16[96,768]{1,0:T(8,128)(2,1)S(1)}, u32[]{:S(2)}, u32[]{:S(2)}) %collective-permute-start.12) | collective-permute-done | bytes 147488 | tf_op jit(solution)/shard_map/ppermute | solution.py:15
  17.2 2.0 %collective-permute-start.2 = (bf16[128,768]{1,0:T(8,128)(2,1)S(1)}, bf16[128,768]{1,0:T(8,128)(2,1)S(1)}, u32[]{:S(2)}, u32[]{:S(2)}) collective-permute-start(bf16[128,768]{1,0:T(8,128)(2,1)S(1)} %get-tuple-element.18), channel_id=1, source_target_pairs={{0,4},{4,0},{8,12},{12,8},{1,5},{5,1},{9,13},{13,9},{2,6},{6,2},{1... | collective-permute-start | bytes 589832 | tf_op jit(solution)/shard_map/ppermute | solution.py:15
  19.2 1.6 %collective-permute-done.8.refs_2_ = bf16[112,768]{1,0:T(8,128)(2,1)S(1)} collective-permute-done((bf16[112,768]{1,0:T(8,128)(2,1)S(1)}, bf16[112,768]{1,0:T(8,128)(2,1)S(1)}, u32[]{:S(2)}, u32[]{:S(2)}) %collective-permute-start.8) | collective-permute-done | bytes 172064 | tf_op jit(solution)/shard_map/ppermute | solution.py:15
  20.9 2.0 %collective-permute-start.7 = (bf16[112,768]{1,0:T(8,128)(2,1)S(1)}, bf16[112,768]{1,0:T(8,128)(2,1)S(1)}, u32[]{:S(2)}, u32[]{:S(2)}) collective-permute-start(bf16[112,768]{1,0:T(8,128)(2,1)S(1)} %collective-permute-done.6.refs_0_), channel_id=1, source_target_pairs={{0,16},{16,0},{1,17},{17,1},{2,18},{18,2},{3,19},{19,3},{4,20},{20... | collective-permute-start | bytes 516104 | tf_op jit(solution)/shard_map/ppermute | solution.py:15
  22.8 1.7 %collective-permute-done.10.refs_4_ = bf16[112,768]{1,0:T(8,128)(2,1)S(1)} collective-permute-done((bf16[112,768]{1,0:T(8,128)(2,1)S(1)}, bf16[112,768]{1,0:T(8,128)(2,1)S(1)}, u32[]{:S(2)}, u32[]{:S(2)}) %collective-permute-start.10) | collective-permute-done | bytes 172064 | tf_op jit(solution)/shard_map/ppermute | solution.py:15
  24.6 2.0 %collective-permute-start.9 = (bf16[112,768]{1,0:T(8,128)(2,1)S(1)}, bf16[112,768]{1,0:T(8,128)(2,1)S(1)}, u32[]{:S(2)}, u32[]{:S(2)}) collective-permute-start(bf16[112,768]{1,0:T(8,128)(2,1)S(1)} %collective-permute-done.8.refs_2_), channel_id=1, source_target_pairs={{0,16},{16,0},{1,17},{17,1},{2,18},{18,2},{3,19},{19,3},{4,20},{20... | collective-permute-start | bytes 516104 | tf_op jit(solution)/shard_map/ppermute | solution.py:15
  26.6 2.2 %collective-permute-done.2.refs_2_ = bf16[128,768]{1,0:T(8,128)(2,1)S(1)} collective-permute-done((bf16[128,768]{1,0:T(8,128)(2,1)S(1)}, bf16[128,768]{1,0:T(8,128)(2,1)S(1)}, u32[]{:S(2)}, u32[]{:S(2)}) %collective-permute-start.2) | collective-permute-done | bytes 196640 | tf_op jit(solution)/shard_map/ppermute | solution.py:15
  28.8 2.0 %collective-permute-start.1 = (bf16[128,768]{1,0:T(8,128)(2,1)S(1)}, bf16[128,768]{1,0:T(8,128)(2,1)S(1)}, u32[]{:S(2)}, u32[]{:S(2)}) collective-permute-start(bf16[128,768]{1,0:T(8,128)(2,1)S(1)} %collective-permute-done.refs_0_), channel_id=1, source_target_pairs={{0,16},{16,0},{1,17},{17,1},{2,18},{18,2},{3,19},{19,3},{4,20},{20... | collective-permute-start | bytes 589832 | tf_op jit(solution)/shard_map/ppermute | solution.py:15
  32.1 1.7 %collective-permute-start.3 = (bf16[128,768]{1,0:T(8,128)(2,1)S(1)}, bf16[128,768]{1,0:T(8,128)(2,1)S(1)}, u32[]{:S(2)}, u32[]{:S(2)}) collective-permute-start(bf16[128,768]{1,0:T(8,128)(2,1)S(1)} %collective-permute-done.2.refs_2_), channel_id=1, source_target_pairs={{0,16},{16,0},{1,17},{17,1},{2,18},{18,2},{3,19},{19,3},{4,20},{20... | collective-permute-start | bytes 589832 | tf_op jit(solution)/shard_map/ppermute | solution.py:15
  35.5 5.4 %collective-permute-start.13 = (bf16[128,768]{1,0:T(8,128)(2,1)S(1)}, bf16[128,768]{1,0:T(8,128)(2,1)S(1)}, u32[]{:S(2)}, u32[]{:S(2)}) collective-permute-start(bf16[128,768]{1,0:T(8,128)(2,1)S(1)} %bitcast.25), channel_id=1, source_target_pairs={{0,8},{12,4},{1,9},{13,5},{2,10},{14,6},{3,11},{15,7},{16,24},{28,... | collective-permute-start | bytes 589832 | tf_op jit(solution)/shard_map/ppermute | solution.py:250
  41.7 2.2 %collective-permute-done.3.refs_3_ = bf16[128,768]{1,0:T(8,128)(2,1)S(1)} collective-permute-done((bf16[128,768]{1,0:T(8,128)(2,1)S(1)}, bf16[128,768]{1,0:T(8,128)(2,1)S(1)}, u32[]{:S(2)}, u32[]{:S(2)}) %collective-permute-start.3) | collective-permute-done | bytes 196640 | tf_op jit(solution)/shard_map/ppermute | solution.py:15
  43.9 2.4 %collective-permute-done.5.refs_5_ = bf16[128,768]{1,0:T(8,128)(2,1)S(1)} collective-permute-done((bf16[128,768]{1,0:T(8,128)(2,1)S(1)}, bf16[128,768]{1,0:T(8,128)(2,1)S(1)}, u32[]{:S(2)}, u32[]{:S(2)}) %collective-permute-start.5) | collective-permute-done | bytes 196640 | tf_op jit(solution)/shard_map/ppermute | solution.py:15
  49.6 3.2 %collective-permute-start.15 = (bf16[128,768]{1,0:T(8,128)(2,1)S(1)}, bf16[128,768]{1,0:T(8,128)(2,1)S(1)}, u32[]{:S(2)}, u32[]{:S(2)}) collective-permute-start(bf16[128,768]{1,0:T(8,128)(2,1)S(1)} %get-tuple-element.24.refs_10_), channel_id=1, source_target_pairs={{0,1},{1,2},{2,3},{3,0},{4,5},{5,6},{6,7},{7,4},{8,9},{9,10},{10,1... | collective-permute-start | bytes 589832 | tf_op jit(solution)/shard_map/ppermute | solution.py:274
  52.9 1.9 %collective-permute-start.19 = (bf16[128,768]{1,0:T(8,128)(2,1)S(1)}, bf16[128,768]{1,0:T(8,128)(2,1)S(1)}, u32[]{:S(2)}, u32[]{:S(2)}) collective-permute-start(bf16[128,768]{1,0:T(8,128)(2,1)S(1)} %shard_map.77.refs_9_), channel_id=1, source_target_pairs={{0,1},{1,2},{2,3},{4,5},{5,6},{6,7},{8,9},{9,10},{10,11},{12,13},{... | collective-permute-start | bytes 589832 | tf_op jit(solution)/shard_map/ppermute | solution.py:274
  55.0 9.3 %collective-permute-done.16.refs_2_ = bf16[128,768]{1,0:T(8,128)(2,1)S(1)} collective-permute-done((bf16[128,768]{1,0:T(8,128)(2,1)S(1)}, bf16[128,768]{1,0:T(8,128)(2,1)S(1)}, u32[]{:S(2)}, u32[]{:S(2)}) %collective-permute-start.16) | collective-permute-done | bytes 196640 | tf_op jit(solution)/shard_map/ppermute | solution.py:274
  66.0 2.5 %collective-permute-done.20.refs_2_ = bf16[128,768]{1,0:T(8,128)(2,1)S(1)} collective-permute-done((bf16[128,768]{1,0:T(8,128)(2,1)S(1)}, bf16[128,768]{1,0:T(8,128)(2,1)S(1)}, u32[]{:S(2)}, u32[]{:S(2)}) %collective-permute-start.20) | collective-permute-done | bytes 196640 | tf_op jit(solution)/shard_map/ppermute | solution.py:274
  69.7 1.8 %collective-permute-start.22 = (bf16[128,768]{1,0:T(8,128)(2,1)S(1)}, bf16[128,768]{1,0:T(8,128)(2,1)S(1)}, u32[]{:S(2)}, u32[]{:S(2)}) collective-permute-start(bf16[128,768]{1,0:T(8,128)(2,1)S(1)} %shard_map.80.refs_9_), channel_id=1, source_target_pairs={{0,1},{1,2},{2,3},{4,5},{5,6},{6,7},{8,9},{9,10},{10,11},{12,13},{... | collective-permute-start | bytes 589832 | tf_op jit(solution)/shard_map/ppermute | solution.py:274
  71.5 1.9 %collective-permute-start.21 = (bf16[128,768]{1,0:T(8,128)(2,1)S(1)}, bf16[128,768]{1,0:T(8,128)(2,1)S(1)}, u32[]{:S(2)}, u32[]{:S(2)}) collective-permute-start(bf16[128,768]{1,0:T(8,128)(2,1)S(1)} %shard_map.80.refs_9_), channel_id=1, source_target_pairs={{0,9},{1,10},{2,11},{3,8},{4,13},{5,14},{6,15},{7,12},{8,1},{9,2},... | collective-permute-start | bytes 589832 | tf_op jit(solution)/shard_map/ppermute | solution.py:274
  75.1 7.0 %collective-permute-done.23.refs_2_ = bf16[128,768]{1,0:T(8,128)(2,1)S(1)} collective-permute-done((bf16[128,768]{1,0:T(8,128)(2,1)S(1)}, bf16[128,768]{1,0:T(8,128)(2,1)S(1)}, u32[]{:S(2)}, u32[]{:S(2)}) %collective-permute-start.23) | collective-permute-done | bytes 196640 | tf_op jit(solution)/shard_map/ppermute | solution.py:274
  83.3 3.0 %collective-permute-done.21.refs_2_ = bf16[128,768]{1,0:T(8,128)(2,1)S(1)} collective-permute-done((bf16[128,768]{1,0:T(8,128)(2,1)S(1)}, bf16[128,768]{1,0:T(8,128)(2,1)S(1)}, u32[]{:S(2)}, u32[]{:S(2)}) %collective-permute-start.21) | collective-permute-done | bytes 196640 | tf_op jit(solution)/shard_map/ppermute | solution.py:274
  87.9 6.5 %collective-permute-done.25.returned_ref = bf16[128,768]{1,0:T(8,128)(2,1)S(1)} collective-permute-done((bf16[128,768]{1,0:T(8,128)(2,1)S(1)}, bf16[128,768]{1,0:T(8,128)(2,1)S(1)}, u32[]{:S(2)}, u32[]{:S(2)}) %collective-permute-start.25) | collective-permute-done | bytes 196640 | tf_op jit(solution)/shard_map/ppermute | solution.py:15
  (54 shorter events, 18.4 us)
Async XLA Ops:
  1.5 17.7 %collective-permute-start.6 = (bf16[112,768]{1,0:T(8,128)(2,1)S(1)}, bf16[112,768]{1,0:T(8,128)(2,1)S(1)}, u32[]{:S(2)}, u32[]{:S(2)}) collective-permute-start(bf16[112,768]{1,0:T(8,128)(2,1)S(1)} %get-tuple-element.20), channel_id=1, source_target_pairs={{0,4},{4,0},{8,12},{12,8},{1,5},{5,1},{9,13},{13,9},{2,6},{6,2},{1... | collective-permute-start | bytes 516104 | tf_op jit(solution)/shard_map/ppermute | solution.py:15
  5.5 21.0 %collective-permute-start = (bf16[128,768]{1,0:T(8,128)(2,1)S(1)}, bf16[128,768]{1,0:T(8,128)(2,1)S(1)}, u32[]{:S(2)}, u32[]{:S(2)}) collective-permute-start(bf16[128,768]{1,0:T(8,128)(2,1)S(1)} %shard_map.73), channel_id=1, source_target_pairs={{0,4},{4,0},{8,12},{12,8},{1,5},{5,1},{9,13},{13,9},{2,6},{6,2},{1... | collective-permute-start | bytes 589832 | tf_op jit(solution)/shard_map/ppermute | solution.py:15
  5.8 11.4 %collective-permute-start.12 = (bf16[96,768]{1,0:T(8,128)(2,1)S(1)}, bf16[96,768]{1,0:T(8,128)(2,1)S(1)}, u32[]{:S(2)}, u32[]{:S(2)}) collective-permute-start(bf16[96,768]{1,0:T(8,128)(2,1)S(1)} %get-tuple-element.23), channel_id=1, source_target_pairs={{0,4},{4,0},{8,12},{12,8},{1,5},{5,1},{9,13},{13,9},{2,6},{6,2},{1... | collective-permute-start | bytes 442376 | tf_op jit(solution)/shard_map/ppermute | solution.py:15
  7.6 13.2 %collective-permute-start.8 = (bf16[112,768]{1,0:T(8,128)(2,1)S(1)}, bf16[112,768]{1,0:T(8,128)(2,1)S(1)}, u32[]{:S(2)}, u32[]{:S(2)}) collective-permute-start(bf16[112,768]{1,0:T(8,128)(2,1)S(1)} %get-tuple-element.21), channel_id=1, source_target_pairs={{0,4},{4,0},{8,12},{12,8},{1,5},{5,1},{9,13},{13,9},{2,6},{6,2},{1... | collective-permute-start | bytes 516104 | tf_op jit(solution)/shard_map/ppermute | solution.py:15
  7.8 16.8 %collective-permute-start.10 = (bf16[112,768]{1,0:T(8,128)(2,1)S(1)}, bf16[112,768]{1,0:T(8,128)(2,1)S(1)}, u32[]{:S(2)}, u32[]{:S(2)}) collective-permute-start(bf16[112,768]{1,0:T(8,128)(2,1)S(1)} %get-tuple-element.22), channel_id=1, source_target_pairs={{0,4},{4,0},{8,12},{12,8},{1,5},{5,1},{9,13},{13,9},{2,6},{6,2},{1... | collective-permute-start | bytes 516104 | tf_op jit(solution)/shard_map/ppermute | solution.py:15
  17.2 11.6 %collective-permute-start.2 = (bf16[128,768]{1,0:T(8,128)(2,1)S(1)}, bf16[128,768]{1,0:T(8,128)(2,1)S(1)}, u32[]{:S(2)}, u32[]{:S(2)}) collective-permute-start(bf16[128,768]{1,0:T(8,128)(2,1)S(1)} %get-tuple-element.18), channel_id=1, source_target_pairs={{0,4},{4,0},{8,12},{12,8},{1,5},{5,1},{9,13},{13,9},{2,6},{6,2},{1... | collective-permute-start | bytes 589832 | tf_op jit(solution)/shard_map/ppermute | solution.py:15
  19.2 12.9 %collective-permute-start.4 = (bf16[128,768]{1,0:T(8,128)(2,1)S(1)}, bf16[128,768]{1,0:T(8,128)(2,1)S(1)}, u32[]{:S(2)}, u32[]{:S(2)}) collective-permute-start(bf16[128,768]{1,0:T(8,128)(2,1)S(1)} %get-tuple-element.19), channel_id=1, source_target_pairs={{0,4},{4,0},{8,12},{12,8},{1,5},{5,1},{9,13},{13,9},{2,6},{6,2},{1... | collective-permute-start | bytes 589832 | tf_op jit(solution)/shard_map/ppermute | solution.py:15
  20.9 12.9 %collective-permute-start.7 = (bf16[112,768]{1,0:T(8,128)(2,1)S(1)}, bf16[112,768]{1,0:T(8,128)(2,1)S(1)}, u32[]{:S(2)}, u32[]{:S(2)}) collective-permute-start(bf16[112,768]{1,0:T(8,128)(2,1)S(1)} %collective-permute-done.6.refs_0_), channel_id=1, source_target_pairs={{0,16},{16,0},{1,17},{17,1},{2,18},{18,2},{3,19},{19,3},{4,20},{20... | collective-permute-start | bytes 516104 | tf_op jit(solution)/shard_map/ppermute | solution.py:15
  24.6 9.6 %collective-permute-start.9 = (bf16[112,768]{1,0:T(8,128)(2,1)S(1)}, bf16[112,768]{1,0:T(8,128)(2,1)S(1)}, u32[]{:S(2)}, u32[]{:S(2)}) collective-permute-start(bf16[112,768]{1,0:T(8,128)(2,1)S(1)} %collective-permute-done.8.refs_2_), channel_id=1, source_target_pairs={{0,16},{16,0},{1,17},{17,1},{2,18},{18,2},{3,19},{19,3},{4,20},{20... | collective-permute-start | bytes 516104 | tf_op jit(solution)/shard_map/ppermute | solution.py:15
  28.8 12.9 %collective-permute-start.1 = (bf16[128,768]{1,0:T(8,128)(2,1)S(1)}, bf16[128,768]{1,0:T(8,128)(2,1)S(1)}, u32[]{:S(2)}, u32[]{:S(2)}) collective-permute-start(bf16[128,768]{1,0:T(8,128)(2,1)S(1)} %collective-permute-done.refs_0_), channel_id=1, source_target_pairs={{0,16},{16,0},{1,17},{17,1},{2,18},{18,2},{3,19},{19,3},{4,20},{20... | collective-permute-start | bytes 589832 | tf_op jit(solution)/shard_map/ppermute | solution.py:15
  32.1 11.8 %collective-permute-start.3 = (bf16[128,768]{1,0:T(8,128)(2,1)S(1)}, bf16[128,768]{1,0:T(8,128)(2,1)S(1)}, u32[]{:S(2)}, u32[]{:S(2)}) collective-permute-start(bf16[128,768]{1,0:T(8,128)(2,1)S(1)} %collective-permute-done.2.refs_2_), channel_id=1, source_target_pairs={{0,16},{16,0},{1,17},{17,1},{2,18},{18,2},{3,19},{19,3},{4,20},{20... | collective-permute-start | bytes 589832 | tf_op jit(solution)/shard_map/ppermute | solution.py:15
  33.8 12.5 %collective-permute-start.5 = (bf16[128,768]{1,0:T(8,128)(2,1)S(1)}, bf16[128,768]{1,0:T(8,128)(2,1)S(1)}, u32[]{:S(2)}, u32[]{:S(2)}) collective-permute-start(bf16[128,768]{1,0:T(8,128)(2,1)S(1)} %collective-permute-done.4.refs_4_), channel_id=1, source_target_pairs={{0,16},{16,0},{1,17},{17,1},{2,18},{18,2},{3,19},{19,3},{4,20},{20... | collective-permute-start | bytes 589832 | tf_op jit(solution)/shard_map/ppermute | solution.py:15
  34.2 12.2 %collective-permute-start.14 = (bf16[128,768]{1,0:T(8,128)(2,1)S(1)}, bf16[128,768]{1,0:T(8,128)(2,1)S(1)}, u32[]{:S(2)}, u32[]{:S(2)}) collective-permute-start(bf16[128,768]{1,0:T(8,128)(2,1)S(1)} %bitcast.24), channel_id=1, source_target_pairs={{4,12},{8,0},{5,13},{9,1},{6,14},{10,2},{7,15},{11,3},{20,28},{24,... | collective-permute-start | bytes 589832 | tf_op jit(solution)/shard_map/ppermute | solution.py:250
  35.5 10.9 %collective-permute-start.13 = (bf16[128,768]{1,0:T(8,128)(2,1)S(1)}, bf16[128,768]{1,0:T(8,128)(2,1)S(1)}, u32[]{:S(2)}, u32[]{:S(2)}) collective-permute-start(bf16[128,768]{1,0:T(8,128)(2,1)S(1)} %bitcast.25), channel_id=1, source_target_pairs={{0,8},{12,4},{1,9},{13,5},{2,10},{14,6},{3,11},{15,7},{16,24},{28,... | collective-permute-start | bytes 589832 | tf_op jit(solution)/shard_map/ppermute | solution.py:250
  47.6 16.8 %collective-permute-start.16 = (bf16[128,768]{1,0:T(8,128)(2,1)S(1)}, bf16[128,768]{1,0:T(8,128)(2,1)S(1)}, u32[]{:S(2)}, u32[]{:S(2)}) collective-permute-start(bf16[128,768]{1,0:T(8,128)(2,1)S(1)} %shard_map.77.refs_9_), channel_id=1, source_target_pairs={{0,9},{1,10},{2,11},{3,8},{4,13},{5,14},{6,15},{7,12},{8,1},{9,2},... | collective-permute-start | bytes 589832 | tf_op jit(solution)/shard_map/ppermute | solution.py:274
  49.6 14.7 %collective-permute-start.15 = (bf16[128,768]{1,0:T(8,128)(2,1)S(1)}, bf16[128,768]{1,0:T(8,128)(2,1)S(1)}, u32[]{:S(2)}, u32[]{:S(2)}) collective-permute-start(bf16[128,768]{1,0:T(8,128)(2,1)S(1)} %get-tuple-element.24.refs_10_), channel_id=1, source_target_pairs={{0,1},{1,2},{2,3},{3,0},{4,5},{5,6},{6,7},{7,4},{8,9},{9,10},{10,1... | collective-permute-start | bytes 589832 | tf_op jit(solution)/shard_map/ppermute | solution.py:274
  52.9 13.1 %collective-permute-start.19 = (bf16[128,768]{1,0:T(8,128)(2,1)S(1)}, bf16[128,768]{1,0:T(8,128)(2,1)S(1)}, u32[]{:S(2)}, u32[]{:S(2)}) collective-permute-start(bf16[128,768]{1,0:T(8,128)(2,1)S(1)} %shard_map.77.refs_9_), channel_id=1, source_target_pairs={{0,1},{1,2},{2,3},{4,5},{5,6},{6,7},{8,9},{9,10},{10,11},{12,13},{... | collective-permute-start | bytes 589832 | tf_op jit(solution)/shard_map/ppermute | solution.py:274
  54.8 13.7 %collective-permute-start.20 = (bf16[128,768]{1,0:T(8,128)(2,1)S(1)}, bf16[128,768]{1,0:T(8,128)(2,1)S(1)}, u32[]{:S(2)}, u32[]{:S(2)}) collective-permute-start(bf16[128,768]{1,0:T(8,128)(2,1)S(1)} %get-tuple-element.27), channel_id=1, source_target_pairs={{0,9},{1,10},{2,11},{3,8},{4,13},{5,14},{6,15},{7,12},{8,1},{9,2},... | collective-permute-start | bytes 589832 | tf_op jit(solution)/shard_map/ppermute | solution.py:274
  65.5 16.6 %collective-permute-start.23 = (bf16[128,768]{1,0:T(8,128)(2,1)S(1)}, bf16[128,768]{1,0:T(8,128)(2,1)S(1)}, u32[]{:S(2)}, u32[]{:S(2)}) collective-permute-start(bf16[128,768]{1,0:T(8,128)(2,1)S(1)} %get-tuple-element.28), channel_id=1, source_target_pairs={{0,9},{1,10},{2,11},{3,8},{4,13},{5,14},{6,15},{7,12},{8,1},{9,2},... | collective-permute-start | bytes 589832 | tf_op jit(solution)/shard_map/ppermute | solution.py:274
  69.7 12.4 %collective-permute-start.22 = (bf16[128,768]{1,0:T(8,128)(2,1)S(1)}, bf16[128,768]{1,0:T(8,128)(2,1)S(1)}, u32[]{:S(2)}, u32[]{:S(2)}) collective-permute-start(bf16[128,768]{1,0:T(8,128)(2,1)S(1)} %shard_map.80.refs_9_), channel_id=1, source_target_pairs={{0,1},{1,2},{2,3},{4,5},{5,6},{6,7},{8,9},{9,10},{10,11},{12,13},{... | collective-permute-start | bytes 589832 | tf_op jit(solution)/shard_map/ppermute | solution.py:274
  71.5 14.8 %collective-permute-start.21 = (bf16[128,768]{1,0:T(8,128)(2,1)S(1)}, bf16[128,768]{1,0:T(8,128)(2,1)S(1)}, u32[]{:S(2)}, u32[]{:S(2)}) collective-permute-start(bf16[128,768]{1,0:T(8,128)(2,1)S(1)} %shard_map.80.refs_9_), channel_id=1, source_target_pairs={{0,9},{1,10},{2,11},{3,8},{4,13},{5,14},{6,15},{7,12},{8,1},{9,2},... | collective-permute-start | bytes 589832 | tf_op jit(solution)/shard_map/ppermute | solution.py:274
  73.4 12.9 %collective-permute-start.18 = (bf16[128,768]{1,0:T(8,128)(2,1)S(1)}, bf16[128,768]{1,0:T(8,128)(2,1)S(1)}, u32[]{:S(2)}, u32[]{:S(2)}) collective-permute-start(bf16[128,768]{1,0:T(8,128)(2,1)S(1)} %get-tuple-element.26.refs_9_), channel_id=1, source_target_pairs={{0,1},{1,2},{2,3},{3,0},{4,5},{5,6},{6,7},{7,4},{8,9},{9,10},{10,1... | collective-permute-start | bytes 589832 | tf_op jit(solution)/shard_map/ppermute | solution.py:274
  73.8 14.1 %collective-permute-start.17 = (bf16[128,768]{1,0:T(8,128)(2,1)S(1)}, bf16[128,768]{1,0:T(8,128)(2,1)S(1)}, u32[]{:S(2)}, u32[]{:S(2)}) collective-permute-start(bf16[128,768]{1,0:T(8,128)(2,1)S(1)} %get-tuple-element.25), channel_id=1, source_target_pairs={{1,0},{2,1},{3,2},{0,3},{5,4},{6,5},{7,6},{4,7},{9,8},{10,9},{11,1... | collective-permute-start | bytes 589832 | tf_op jit(solution)/shard_map/ppermute | solution.py:277
  83.2 11.2 %collective-permute-start.25 = (bf16[128,768]{1,0:T(8,128)(2,1)S(1)}, bf16[128,768]{1,0:T(8,128)(2,1)S(1)}, u32[]{:S(2)}, u32[]{:S(2)}) collective-permute-start(bf16[128,768]{1,0:T(8,128)(2,1)S(1)} %shard_map.81.refs_10_), channel_id=1, source_target_pairs={{0,8},{4,12},{8,0},{12,4},{1,9},{5,13},{9,1},{13,5},{2,10},{6,14},... | collective-permute-start | bytes 589832 | tf_op jit(solution)/shard_map/ppermute | solution.py:15
  (9 other events, 287.4 us)

commit v3 on v2

--- a/solution.py
+++ b/solution.py
@@ -160,22 +160,33 @@
         if which == 0:
             outs[1][...] = x.astype(jnp.bfloat16)
             x = jnp.where(leg == 0, fresh_ref[tick - 1].astype(jnp.float32), x)
-    inv_rms = lax.rsqrt(jnp.mean(x * x, axis=-1, keepdims=True) + 1e-06)
-    normed = (x * inv_rms * gain_ref[...]).astype(jnp.bfloat16)
-    columns = columns_ref[...].astype(jnp.float32)
-    column = jnp.where(lax.axis_index("expert") // 2 == 0, columns[0:1], columns[1:2])
-    logit = jnp.sum(normed.astype(jnp.float32) * column, axis=-1, keepdims=True)
-    hidden = []
-    for ref in (up_ref, far_up_ref):
-        up = jnp.dot(normed, ref[...], preferred_element_type=jnp.float32)
-        hidden.append(jnp.maximum(up, 0.0).astype(jnp.bfloat16))
-    out = jnp.dot(hidden[0], down_ref[...], preferred_element_type=jnp.float32)
-    out = out + jnp.dot(hidden[1], far_down_ref[...], preferred_element_type=jnp.float32)
-    y = x + jax.nn.sigmoid(logit) * out
-    y = jnp.where(mask_ref[tick : tick + 1, :1] != 0, y, 0.0).astype(jnp.bfloat16)
-    outs[0][...] = y
-    if which == 0 and tick < last_tick:
-        outs[-1][...] = jnp.where(leg == lax.axis_size("section") - 1, fresh_ref[tick], y)
+    sent = outs[-1] if which == 0 and tick < last_tick else None
+
+    def give(y):
+        outs[0][...] = y
+        if sent is not None:
+            sent[...] = jnp.where(leg == lax.axis_size("section") - 1, fresh_ref[tick], y)
+
+    serves = jnp.max(mask_ref[tick : tick + 1, :]) != 0
+
+    @pl.when(serves)
+    def _():
+        inv_rms = lax.rsqrt(jnp.mean(x * x, axis=-1, keepdims=True) + 1e-06)
+        normed = (x * inv_rms * gain_ref[...]).astype(jnp.bfloat16)
+        columns = columns_ref[...].astype(jnp.float32)
+        column = jnp.where(lax.axis_index("expert") // 2 == 0, columns[0:1], columns[1:2])
+        logit = jnp.sum(normed.astype(jnp.float32) * column, axis=-1, keepdims=True)
+        hidden = []
+        for ref in (up_ref, far_up_ref):
+            up = jnp.dot(normed, ref[...], preferred_element_type=jnp.float32)
+            hidden.append(jnp.maximum(up, 0.0).astype(jnp.bfloat16))
+        out = jnp.dot(hidden[0], down_ref[...], preferred_element_type=jnp.float32)
+        out = out + jnp.dot(hidden[1], far_down_ref[...], preferred_element_type=jnp.float32)
+        give((x + jax.nn.sigmoid(logit) * out).astype(jnp.bfloat16))
+
+    @pl.when(jnp.logical_not(serves))
+    def _():
+        give(jnp.zeros(x.shape, jnp.bfloat16))
 
 
 def gather_kernel(first_ref, second_ref, own_ref, returned_ref, out_ref):
@@ -247,7 +258,7 @@
     own_rows = pending_microgroups[0]
     other_rows = []
     for senders in ((0, places - 1), range(1, places - 1)):
-        other_rows.append(lax.ppermute(own_rows, "expert", [(e, e ^ 2) for e in senders]))
+        other_rows.append(lax.ppermute(own_rows, "expert", [(e, places - 1 - e) for e in senders]))
     rows_shape = jax.ShapeDtypeStruct((num_rows, width), jnp.bfloat16)
 
     def layer(tick, which, inputs, after):
@@ -267,7 +278,7 @@
     def ahead(value, flip, wrap):
         last = legs if wrap else legs - 1
         perm = [
-            (e * legs + s, (e ^ flip) * legs + (s + 1) % legs)
+            (e * legs + s, (places - 1 - e if flip else e) * legs + (s + 1) % legs)
             for e in range(places)
             for s in range(last)
         ]
@@ -287,10 +298,11 @@
             got = layer(tick, which, current[which], after)
             after = done[which] = got[0]
             if tick + 1 < TICKS:
-                following[1 - which] = ahead(got[-1], 2, True)
-                straight[which] = ahead(got[0], 0, which == 0)
+                following[1 - which] = ahead(got[-1], True, True)
+                straight[which] = ahead(got[0], False, which == 0)
             elif which == 1:
-                returned = swapped(got[0], "expert", 1)
+                mirror = [(e, places - 1 - e) for e in range(places)]
+                returned = lax.ppermute(got[0], "expert", mirror)
             if tick and which == 0:
                 outputs.append(back(got[1]))
         if tick + 1 < TICKS:

time: 95.8 us -> 104 us (1.086)
  the two profiles are of different devices: /device:TPU:0 before, /device:TPU:13 now
where the time goes in v3:
time: 104 us; the launch traced here: 103 us
  waiting for transfers between devices  55.5 us (53%)
  starting transfers between devices  35.3 us (34%)
  Pallas kernels  12.1 us (12%)
    ppermute x13, waiting for transfers between devices, swapped(): lax.ppermute(x, axis, [(i, i ^ 1 << bit) for i in range(lax.axis_size(axi...  28.4 us
    ppermute x8, starting transfers between devices, ahead(): return lax.ppermute(value, ('expert', 'section'), perm)  22.8 us
    ppermute x8, waiting for transfers between devices, ahead(): return lax.ppermute(value, ('expert', 'section'), perm)  21.3 us
    ppermute x13, starting transfers between devices, swapped(): lax.ppermute(x, axis, [(i, i ^ 1 << bit) for i in range(lax.axis_size(axi...  8.08 us
    pallas_call x6, Pallas kernels, layer(): pl.pallas_call(functools.partial(layer_kernel, tick, which, TICKS - 1), o...  7.93 us
    ppermute x2, waiting for transfers between devices, back(): lax.ppermute(value, 'section', [((s + 1) % legs, s) for s in range(legs)])  5.55 us
    ppermute x2, starting transfers between devices, pairs_per_device(): lax.ppermute(own_rows, 'expert', [(e, places - 1 - e) for e in senders])  3.87 us
    pallas_call x2, Pallas kernels, cut(): pl.pallas_call(functools.partial(cut_kernel, some), out_shape=[pltpu.VMEM...  2.5 us
  transfers between devices with their start and end apart: 26, of which 13 were waited for; matrix products, arithmetic and copies ran while one was open for 0% of the time, Pallas kernels for 8%

profile of v3, /device:TPU:13, one launch (start us, length us, event | category | flops | bytes accessed | tf_op | source)
XLA Modules:
  0.0 103.3 jit_solution(12446851917453575323)
XLA Ops:
  0.0 1.4 %shard_map.74 = (bf16[128,768]{1,0:T(8,128)(2,1)S(1)}, bf16[128,768]{1,0:T(8,128)(2,1)S(1)}, bf16[112,768]{1,0:T(8,128)(2,1)S(1)}, bf16[112,768]{1,0:T(8,128)(2,...) custom-call(bf16[768,768]{1,0:T(8,128)(2,1)} %bitcast.6, bf16[768,768]{1,0:T(8,128)(2,1)} %bitcast.15), custom_call_target="tpu_custom_call" | custom-call | tf_op jit(solution)/shard_map/pallas_call | solution.py:219
  5.8 8.3 %collective-permute-done.12.refs_6_ = bf16[96,768]{1,0:T(8,128)(2,1)S(1)} collective-permute-done((bf16[96,768]{1,0:T(8,128)(2,1)S(1)}, bf16[96,768]{1,0:T(8,128)(2,1)S(1)}, u32[]{:S(2)}, u32[]{:S(2)}) %collective-permute-start.12) | collective-permute-done | bytes 147488 | tf_op jit(solution)/shard_map/ppermute | solution.py:15
  15.6 2.2 %collective-permute-done.8.refs_2_ = bf16[112,768]{1,0:T(8,128)(2,1)S(1)} collective-permute-done((bf16[112,768]{1,0:T(8,128)(2,1)S(1)}, bf16[112,768]{1,0:T(8,128)(2,1)S(1)}, u32[]{:S(2)}, u32[]{:S(2)}) %collective-permute-start.8) | collective-permute-done | bytes 172064 | tf_op jit(solution)/shard_map/ppermute | solution.py:15
  18.1 3.5 %collective-permute-done.10.refs_4_ = bf16[112,768]{1,0:T(8,128)(2,1)S(1)} collective-permute-done((bf16[112,768]{1,0:T(8,128)(2,1)S(1)}, bf16[112,768]{1,0:T(8,128)(2,1)S(1)}, u32[]{:S(2)}, u32[]{:S(2)}) %collective-permute-start.10) | collective-permute-done | bytes 172064 | tf_op jit(solution)/shard_map/ppermute | solution.py:15
  23.0 2.7 %collective-permute-done.2.refs_2_ = bf16[128,768]{1,0:T(8,128)(2,1)S(1)} collective-permute-done((bf16[128,768]{1,0:T(8,128)(2,1)S(1)}, bf16[128,768]{1,0:T(8,128)(2,1)S(1)}, u32[]{:S(2)}, u32[]{:S(2)}) %collective-permute-start.2) | collective-permute-done | bytes 196640 | tf_op jit(solution)/shard_map/ppermute | solution.py:15
  26.0 4.0 %collective-permute-done.4.refs_4_ = bf16[128,768]{1,0:T(8,128)(2,1)S(1)} collective-permute-done((bf16[128,768]{1,0:T(8,128)(2,1)S(1)}, bf16[128,768]{1,0:T(8,128)(2,1)S(1)}, u32[]{:S(2)}, u32[]{:S(2)}) %collective-permute-start.4) | collective-permute-done | bytes 196640 | tf_op jit(solution)/shard_map/ppermute | solution.py:15
  31.4 3.2 %collective-permute-start.14 = (bf16[128,768]{1,0:T(8,128)(2,1)S(1)}, bf16[128,768]{1,0:T(8,128)(2,1)S(1)}, u32[]{:S(2)}, u32[]{:S(2)}) collective-permute-start(bf16[128,768]{1,0:T(8,128)(2,1)S(1)} %bitcast.24), channel_id=1, source_target_pairs={{4,8},{8,4},{5,9},{9,5},{6,10},{10,6},{7,11},{11,7},{20,24},{24,20... | collective-permute-start | bytes 589832 | tf_op jit(solution)/shard_map/ppermute | solution.py:261
  36.1 3.4 %collective-permute-done.3.refs_3_ = bf16[128,768]{1,0:T(8,128)(2,1)S(1)} collective-permute-done((bf16[128,768]{1,0:T(8,128)(2,1)S(1)}, bf16[128,768]{1,0:T(8,128)(2,1)S(1)}, u32[]{:S(2)}, u32[]{:S(2)}) %collective-permute-start.3) | collective-permute-done | bytes 196640 | tf_op jit(solution)/shard_map/ppermute | solution.py:15
  39.5 4.2 %collective-permute-done.5.refs_5_ = bf16[128,768]{1,0:T(8,128)(2,1)S(1)} collective-permute-done((bf16[128,768]{1,0:T(8,128)(2,1)S(1)}, bf16[128,768]{1,0:T(8,128)(2,1)S(1)}, u32[]{:S(2)}, u32[]{:S(2)}) %collective-permute-start.5) | collective-permute-done | bytes 196640 | tf_op jit(solution)/shard_map/ppermute | solution.py:15
  43.8 1.3 %shard_map.77.refs_9_ = bf16[128,768]{1,0:T(8,128)(2,1)S(1)} custom-call(s32[8,128]{1,0:T(8,128)S(1)} %mask.1.refs_0_, bf16[128,768]{1,0:T(8,128)(2,1)S(1)} %collective-permute-done.13.refs_1_, bf16[128,768]{1,0:T(8,128)(2,1)S(1)} %collective-permute-done.14.refs_2_, f32[1,768]{1,0:T(1,128)S(1)} %copy-done.4, bf16[2,768]{1,0:T(2,128)(2,1)S(1)} %bitcast.29, ...), custom_call_target="tpu_custom_call" | custom-call | tf_op jit(solution)/shard_map/pallas_call | solution.py:270
  45.1 3.3 %collective-permute-start.16 = (bf16[128,768]{1,0:T(8,128)(2,1)S(1)}, bf16[128,768]{1,0:T(8,128)(2,1)S(1)}, u32[]{:S(2)}, u32[]{:S(2)}) collective-permute-start(bf16[128,768]{1,0:T(8,128)(2,1)S(1)} %shard_map.77.refs_9_), channel_id=1, source_target_pairs={{0,13},{1,14},{2,15},{3,12},{4,9},{5,10},{6,11},{7,8},{8,5},{9,6},... | collective-permute-start | bytes 589832 | tf_op jit(solution)/shard_map/ppermute | solution.py:285
  48.4 1.3 %shard_map.78 = (bf16[128,768]{1,0:T(8,128)(2,1)S(1)}, bf16[128,768]{1,0:T(8,128)(2,1)S(1)}) custom-call(s32[8,128]{1,0:T(8,128)S(1)} %mask.1.refs_0_, bf16[128,768]{1,0:T(8,128)(2,1)S(1)} %bitcast.27, bf16[2,128,768]{2,1,0:T(8,128)(2,1)S(1)} %copy-done.2, f32[1,768]{1,0:T(1,128)S(1)} %copy-done.4, bf16[2,768]{1,0:T(2,128)(2,1)S(1)} %bitcast.30, ...), custom_call_target="tpu_custom_call" | custom-call | tf_op jit(solution)/shard_map/pallas_call | solution.py:270
  49.9 3.6 %collective-permute-start.19 = (bf16[128,768]{1,0:T(8,128)(2,1)S(1)}, bf16[128,768]{1,0:T(8,128)(2,1)S(1)}, u32[]{:S(2)}, u32[]{:S(2)}) collective-permute-start(bf16[128,768]{1,0:T(8,128)(2,1)S(1)} %shard_map.77.refs_9_), channel_id=1, source_target_pairs={{0,1},{1,2},{2,3},{4,5},{5,6},{6,7},{8,9},{9,10},{10,11},{12,13},{... | collective-permute-start | bytes 589832 | tf_op jit(solution)/shard_map/ppermute | solution.py:285
  53.5 11.8 %collective-permute-done.16.refs_2_ = bf16[128,768]{1,0:T(8,128)(2,1)S(1)} collective-permute-done((bf16[128,768]{1,0:T(8,128)(2,1)S(1)}, bf16[128,768]{1,0:T(8,128)(2,1)S(1)}, u32[]{:S(2)}, u32[]{:S(2)}) %collective-permute-start.16) | collective-permute-done | bytes 196640 | tf_op jit(solution)/shard_map/ppermute | solution.py:285
  65.3 1.3 %shard_map.79 = (bf16[128,768]{1,0:T(8,128)(2,1)S(1)}, bf16[128,768]{1,0:T(8,128)(2,1)S(1)}, bf16[128,768]{1,0:T(8,128)(2,1)S(1)}) custom-call(s32[8,128]{1,0:T(8,128)S(1)} %mask.1.refs_0_, bf16[128,768]{1,0:T(8,128)(2,1)S(1)} %collective-permute-done.15.refs_1_, bf16[128,768]{1,0:T(8,128)(2,1)S(1)} %collective-permute-done.16.refs_2_, ...), custom_call_target="tpu_custom_call" | custom-call | tf_op jit(solution)/shard_map/pallas_call | solution.py:270
  66.7 2.3 %collective-permute-start.23 = (bf16[128,768]{1,0:T(8,128)(2,1)S(1)}, bf16[128,768]{1,0:T(8,128)(2,1)S(1)}, u32[]{:S(2)}, u32[]{:S(2)}) collective-permute-start(bf16[128,768]{1,0:T(8,128)(2,1)S(1)} %get-tuple-element.28), channel_id=1, source_target_pairs={{0,13},{1,14},{2,15},{3,12},{4,9},{5,10},{6,11},{7,8},{8,5},{9,6},... | collective-permute-start | bytes 589832 | tf_op jit(solution)/shard_map/ppermute | solution.py:285
  69.0 1.4 %collective-permute-done.20.refs_2_ = bf16[128,768]{1,0:T(8,128)(2,1)S(1)} collective-permute-done((bf16[128,768]{1,0:T(8,128)(2,1)S(1)}, bf16[128,768]{1,0:T(8,128)(2,1)S(1)}, u32[]{:S(2)}, u32[]{:S(2)}) %collective-permute-start.20) | collective-permute-done | bytes 196640 | tf_op jit(solution)/shard_map/ppermute | solution.py:285
  70.4 1.3 %shard_map.80.refs_9_ = bf16[128,768]{1,0:T(8,128)(2,1)S(1)} custom-call(s32[8,128]{1,0:T(8,128)S(1)} %mask.1.refs_0_, bf16[128,768]{1,0:T(8,128)(2,1)S(1)} %collective-permute-done.19.refs_1_, bf16[128,768]{1,0:T(8,128)(2,1)S(1)} %collective-permute-done.20.refs_2_, f32[1,768]{1,0:T(1,128)S(1)} %copy-done.4, bf16[2,768]{1,0:T(2,128)(2,1)S(1)} %bitcast.32, ...), custom_call_target="tpu_custom_call" | custom-call | tf_op jit(solution)/shard_map/pallas_call | solution.py:270
  71.7 13.2 %collective-permute-start.22 = (bf16[128,768]{1,0:T(8,128)(2,1)S(1)}, bf16[128,768]{1,0:T(8,128)(2,1)S(1)}, u32[]{:S(2)}, u32[]{:S(2)}) collective-permute-start(bf16[128,768]{1,0:T(8,128)(2,1)S(1)} %shard_map.80.refs_9_), channel_id=1, source_target_pairs={{0,1},{1,2},{2,3},{4,5},{5,6},{6,7},{8,9},{9,10},{10,11},{12,13},{... | collective-permute-start | bytes 589832 | tf_op jit(solution)/shard_map/ppermute | solution.py:285
  85.6 5.3 %collective-permute-done.22.refs_1_ = bf16[128,768]{1,0:T(8,128)(2,1)S(1)} collective-permute-done((bf16[128,768]{1,0:T(8,128)(2,1)S(1)}, bf16[128,768]{1,0:T(8,128)(2,1)S(1)}, u32[]{:S(2)}, u32[]{:S(2)}) %collective-permute-start.22) | collective-permute-done | bytes 196640 | tf_op jit(solution)/shard_map/ppermute | solution.py:285
  90.9 1.3 %shard_map.81.refs_10_ = bf16[128,768]{1,0:T(8,128)(2,1)S(1)} custom-call(s32[8,128]{1,0:T(8,128)S(1)} %mask.1.refs_0_, bf16[128,768]{1,0:T(8,128)(2,1)S(1)} %collective-permute-done.22.refs_1_, bf16[128,768]{1,0:T(8,128)(2,1)S(1)} %collective-permute-done.23.refs_2_, f32[1,768]{1,0:T(1,128)S(1)} %copy-done.4, bf16[2,768]{1,0:T(2,128)(2,1)S(1)} %bitcast.33, ...), custom_call_target="tpu_custom_call" | custom-call | tf_op jit(solution)/shard_map/pallas_call | solution.py:270
  92.4 2.8 %collective-permute-done.18.refs_1_ = bf16[128,768]{1,0:T(8,128)(2,1)S(1)} collective-permute-done((bf16[128,768]{1,0:T(8,128)(2,1)S(1)}, bf16[128,768]{1,0:T(8,128)(2,1)S(1)}, u32[]{:S(2)}, u32[]{:S(2)}) %collective-permute-start.18) | collective-permute-done | bytes 196640 | tf_op jit(solution)/shard_map/ppermute | solution.py:285
  95.2 1.3 %shard_map.82 = (bf16[128,768]{1,0:T(8,128)(2,1)S(1)}, bf16[128,768]{1,0:T(8,128)(2,1)S(1)}) custom-call(s32[8,128]{1,0:T(8,128)S(1)} %mask.1.refs_0_, bf16[128,768]{1,0:T(8,128)(2,1)S(1)} %collective-permute-done.18.refs_1_, bf16[128,768]{1,0:T(8,128)(2,1)S(1)} %collective-permute-done.21.refs_2_, bf16[2,128,768]{2,1,0:T(8,128)(2,1)S(1)} %copy-done.2, ...), custom_call_target="tpu_custom_call" | custom-call | tf_op jit(solution)/shard_map/pallas_call | solution.py:270
  96.8 5.5 %collective-permute-done.24.second_ref = bf16[128,768]{1,0:T(8,128)(2,1)S(1)} collective-permute-done((bf16[128,768]{1,0:T(8,128)(2,1)S(1)}, bf16[128,768]{1,0:T(8,128)(2,1)S(1)}, u32[]{:S(2)}, u32[]{:S(2)}) %collective-permute-start.24) | collective-permute-done | bytes 196640 | tf_op jit(solution)/shard_map/ppermute | solution.py:288
  (54 shorter events, 12.8 us)
Async XLA Ops:
  1.5 12.9 %collective-permute-start.6 = (bf16[112,768]{1,0:T(8,128)(2,1)S(1)}, bf16[112,768]{1,0:T(8,128)(2,1)S(1)}, u32[]{:S(2)}, u32[]{:S(2)}) collective-permute-start(bf16[112,768]{1,0:T(8,128)(2,1)S(1)} %get-tuple-element.20), channel_id=1, source_target_pairs={{0,4},{4,0},{8,12},{12,8},{1,5},{5,1},{9,13},{13,9},{2,6},{6,2},{1... | collective-permute-start | bytes 516104 | tf_op jit(solution)/shard_map/ppermute | solution.py:15
  2.8 18.9 %collective-permute-start = (bf16[128,768]{1,0:T(8,128)(2,1)S(1)}, bf16[128,768]{1,0:T(8,128)(2,1)S(1)}, u32[]{:S(2)}, u32[]{:S(2)}) collective-permute-start(bf16[128,768]{1,0:T(8,128)(2,1)S(1)} %shard_map.73), channel_id=1, source_target_pairs={{0,4},{4,0},{8,12},{12,8},{1,5},{5,1},{9,13},{13,9},{2,6},{6,2},{1... | collective-permute-start | bytes 589832 | tf_op jit(solution)/shard_map/ppermute | solution.py:15
  4.0 10.2 %collective-permute-start.12 = (bf16[96,768]{1,0:T(8,128)(2,1)S(1)}, bf16[96,768]{1,0:T(8,128)(2,1)S(1)}, u32[]{:S(2)}, u32[]{:S(2)}) collective-permute-start(bf16[96,768]{1,0:T(8,128)(2,1)S(1)} %get-tuple-element.23), channel_id=1, source_target_pairs={{0,4},{4,0},{8,12},{12,8},{1,5},{5,1},{9,13},{13,9},{2,6},{6,2},{1... | collective-permute-start | bytes 442376 | tf_op jit(solution)/shard_map/ppermute | solution.py:15
  4.4 13.5 %collective-permute-start.8 = (bf16[112,768]{1,0:T(8,128)(2,1)S(1)}, bf16[112,768]{1,0:T(8,128)(2,1)S(1)}, u32[]{:S(2)}, u32[]{:S(2)}) collective-permute-start(bf16[112,768]{1,0:T(8,128)(2,1)S(1)} %get-tuple-element.21), channel_id=1, source_target_pairs={{0,4},{4,0},{8,12},{12,8},{1,5},{5,1},{9,13},{13,9},{2,6},{6,2},{1... | collective-permute-start | bytes 516104 | tf_op jit(solution)/shard_map/ppermute | solution.py:15
  5.5 16.1 %collective-permute-start.10 = (bf16[112,768]{1,0:T(8,128)(2,1)S(1)}, bf16[112,768]{1,0:T(8,128)(2,1)S(1)}, u32[]{:S(2)}, u32[]{:S(2)}) collective-permute-start(bf16[112,768]{1,0:T(8,128)(2,1)S(1)} %get-tuple-element.22), channel_id=1, source_target_pairs={{0,4},{4,0},{8,12},{12,8},{1,5},{5,1},{9,13},{13,9},{2,6},{6,2},{1... | collective-permute-start | bytes 516104 | tf_op jit(solution)/shard_map/ppermute | solution.py:15
  14.2 11.6 %collective-permute-start.2 = (bf16[128,768]{1,0:T(8,128)(2,1)S(1)}, bf16[128,768]{1,0:T(8,128)(2,1)S(1)}, u32[]{:S(2)}, u32[]{:S(2)}) collective-permute-start(bf16[128,768]{1,0:T(8,128)(2,1)S(1)} %get-tuple-element.18), channel_id=1, source_target_pairs={{0,4},{4,0},{8,12},{12,8},{1,5},{5,1},{9,13},{13,9},{2,6},{6,2},{1... | collective-permute-start | bytes 589832 | tf_op jit(solution)/shard_map/ppermute | solution.py:15
  14.3 15.6 %collective-permute-start.4 = (bf16[128,768]{1,0:T(8,128)(2,1)S(1)}, bf16[128,768]{1,0:T(8,128)(2,1)S(1)}, u32[]{:S(2)}, u32[]{:S(2)}) collective-permute-start(bf16[128,768]{1,0:T(8,128)(2,1)S(1)} %get-tuple-element.19), channel_id=1, source_target_pairs={{0,4},{4,0},{8,12},{12,8},{1,5},{5,1},{9,13},{13,9},{2,6},{6,2},{1... | collective-permute-start | bytes 589832 | tf_op jit(solution)/shard_map/ppermute | solution.py:15
  17.9 12.3 %collective-permute-start.7 = (bf16[112,768]{1,0:T(8,128)(2,1)S(1)}, bf16[112,768]{1,0:T(8,128)(2,1)S(1)}, u32[]{:S(2)}, u32[]{:S(2)}) collective-permute-start(bf16[112,768]{1,0:T(8,128)(2,1)S(1)} %collective-permute-done.6.refs_0_), channel_id=1, source_target_pairs={{0,16},{16,0},{1,17},{17,1},{2,18},{18,2},{3,19},{19,3},{4,20},{20... | collective-permute-start | bytes 516104 | tf_op jit(solution)/shard_map/ppermute | solution.py:15
  21.5 9.9 %collective-permute-start.9 = (bf16[112,768]{1,0:T(8,128)(2,1)S(1)}, bf16[112,768]{1,0:T(8,128)(2,1)S(1)}, u32[]{:S(2)}, u32[]{:S(2)}) collective-permute-start(bf16[112,768]{1,0:T(8,128)(2,1)S(1)} %collective-permute-done.8.refs_2_), channel_id=1, source_target_pairs={{0,16},{16,0},{1,17},{17,1},{2,18},{18,2},{3,19},{19,3},{4,20},{20... | collective-permute-start | bytes 516104 | tf_op jit(solution)/shard_map/ppermute | solution.py:15
  21.8 12.9 %collective-permute-start.11 = (bf16[112,768]{1,0:T(8,128)(2,1)S(1)}, bf16[112,768]{1,0:T(8,128)(2,1)S(1)}, u32[]{:S(2)}, u32[]{:S(2)}) collective-permute-start(bf16[112,768]{1,0:T(8,128)(2,1)S(1)} %collective-permute-done.10.refs_4_), channel_id=1, source_target_pairs={{0,16},{16,0},{1,17},{17,1},{2,18},{18,2},{3,19},{19,3},{4,20},{20... | collective-permute-start | bytes 516104 | tf_op jit(solution)/shard_map/ppermute | solution.py:15
  25.8 10.3 %collective-permute-start.1 = (bf16[128,768]{1,0:T(8,128)(2,1)S(1)}, bf16[128,768]{1,0:T(8,128)(2,1)S(1)}, u32[]{:S(2)}, u32[]{:S(2)}) collective-permute-start(bf16[128,768]{1,0:T(8,128)(2,1)S(1)} %collective-permute-done.refs_0_), channel_id=1, source_target_pairs={{0,16},{16,0},{1,17},{17,1},{2,18},{18,2},{3,19},{19,3},{4,20},{20... | collective-permute-start | bytes 589832 | tf_op jit(solution)/shard_map/ppermute | solution.py:15
  30.0 9.5 %collective-permute-start.3 = (bf16[128,768]{1,0:T(8,128)(2,1)S(1)}, bf16[128,768]{1,0:T(8,128)(2,1)S(1)}, u32[]{:S(2)}, u32[]{:S(2)}) collective-permute-start(bf16[128,768]{1,0:T(8,128)(2,1)S(1)} %collective-permute-done.2.refs_2_), channel_id=1, source_target_pairs={{0,16},{16,0},{1,17},{17,1},{2,18},{18,2},{3,19},{19,3},{4,20},{20... | collective-permute-start | bytes 589832 | tf_op jit(solution)/shard_map/ppermute | solution.py:15
  30.2 13.5 %collective-permute-start.5 = (bf16[128,768]{1,0:T(8,128)(2,1)S(1)}, bf16[128,768]{1,0:T(8,128)(2,1)S(1)}, u32[]{:S(2)}, u32[]{:S(2)}) collective-permute-start(bf16[128,768]{1,0:T(8,128)(2,1)S(1)} %collective-permute-done.4.refs_4_), channel_id=1, source_target_pairs={{0,16},{16,0},{1,17},{17,1},{2,18},{18,2},{3,19},{19,3},{4,20},{20... | collective-permute-start | bytes 589832 | tf_op jit(solution)/shard_map/ppermute | solution.py:15
  31.4 12.3 %collective-permute-start.14 = (bf16[128,768]{1,0:T(8,128)(2,1)S(1)}, bf16[128,768]{1,0:T(8,128)(2,1)S(1)}, u32[]{:S(2)}, u32[]{:S(2)}) collective-permute-start(bf16[128,768]{1,0:T(8,128)(2,1)S(1)} %bitcast.24), channel_id=1, source_target_pairs={{4,8},{8,4},{5,9},{9,5},{6,10},{10,6},{7,11},{11,7},{20,24},{24,20... | collective-permute-start | bytes 589832 | tf_op jit(solution)/shard_map/ppermute | solution.py:261
  34.7 9.1 %collective-permute-start.13 = (bf16[128,768]{1,0:T(8,128)(2,1)S(1)}, bf16[128,768]{1,0:T(8,128)(2,1)S(1)}, u32[]{:S(2)}, u32[]{:S(2)}) collective-permute-start(bf16[128,768]{1,0:T(8,128)(2,1)S(1)} %bitcast.25), channel_id=1, source_target_pairs={{0,12},{12,0},{1,13},{13,1},{2,14},{14,2},{3,15},{15,3},{16,28},{2... | collective-permute-start | bytes 589832 | tf_op jit(solution)/shard_map/ppermute | solution.py:261
  45.1 20.2 %collective-permute-start.16 = (bf16[128,768]{1,0:T(8,128)(2,1)S(1)}, bf16[128,768]{1,0:T(8,128)(2,1)S(1)}, u32[]{:S(2)}, u32[]{:S(2)}) collective-permute-start(bf16[128,768]{1,0:T(8,128)(2,1)S(1)} %shard_map.77.refs_9_), channel_id=1, source_target_pairs={{0,13},{1,14},{2,15},{3,12},{4,9},{5,10},{6,11},{7,8},{8,5},{9,6},... | collective-permute-start | bytes 589832 | tf_op jit(solution)/shard_map/ppermute | solution.py:285
  49.8 15.6 %collective-permute-start.15 = (bf16[128,768]{1,0:T(8,128)(2,1)S(1)}, bf16[128,768]{1,0:T(8,128)(2,1)S(1)}, u32[]{:S(2)}, u32[]{:S(2)}) collective-permute-start(bf16[128,768]{1,0:T(8,128)(2,1)S(1)} %get-tuple-element.24.refs_10_), channel_id=1, source_target_pairs={{0,1},{1,2},{2,3},{3,0},{4,5},{5,6},{6,7},{7,4},{8,9},{9,10},{10,1... | collective-permute-start | bytes 589832 | tf_op jit(solution)/shard_map/ppermute | solution.py:285
  49.9 19.1 %collective-permute-start.19 = (bf16[128,768]{1,0:T(8,128)(2,1)S(1)}, bf16[128,768]{1,0:T(8,128)(2,1)S(1)}, u32[]{:S(2)}, u32[]{:S(2)}) collective-permute-start(bf16[128,768]{1,0:T(8,128)(2,1)S(1)} %shard_map.77.refs_9_), channel_id=1, source_target_pairs={{0,1},{1,2},{2,3},{4,5},{5,6},{6,7},{8,9},{9,10},{10,11},{12,13},{... | collective-permute-start | bytes 589832 | tf_op jit(solution)/shard_map/ppermute | solution.py:285
  53.5 17.0 %collective-permute-start.20 = (bf16[128,768]{1,0:T(8,128)(2,1)S(1)}, bf16[128,768]{1,0:T(8,128)(2,1)S(1)}, u32[]{:S(2)}, u32[]{:S(2)}) collective-permute-start(bf16[128,768]{1,0:T(8,128)(2,1)S(1)} %get-tuple-element.27), channel_id=1, source_target_pairs={{0,13},{1,14},{2,15},{3,12},{4,9},{5,10},{6,11},{7,8},{8,5},{9,6},... | collective-permute-start | bytes 589832 | tf_op jit(solution)/shard_map/ppermute | solution.py:285
  66.7 18.9 %collective-permute-start.23 = (bf16[128,768]{1,0:T(8,128)(2,1)S(1)}, bf16[128,768]{1,0:T(8,128)(2,1)S(1)}, u32[]{:S(2)}, u32[]{:S(2)}) collective-permute-start(bf16[128,768]{1,0:T(8,128)(2,1)S(1)} %get-tuple-element.28), channel_id=1, source_target_pairs={{0,13},{1,14},{2,15},{3,12},{4,9},{5,10},{6,11},{7,8},{8,5},{9,6},... | collective-permute-start | bytes 589832 | tf_op jit(solution)/shard_map/ppermute | solution.py:285
  71.7 19.2 %collective-permute-start.22 = (bf16[128,768]{1,0:T(8,128)(2,1)S(1)}, bf16[128,768]{1,0:T(8,128)(2,1)S(1)}, u32[]{:S(2)}, u32[]{:S(2)}) collective-permute-start(bf16[128,768]{1,0:T(8,128)(2,1)S(1)} %shard_map.80.refs_9_), channel_id=1, source_target_pairs={{0,1},{1,2},{2,3},{4,5},{5,6},{6,7},{8,9},{9,10},{10,11},{12,13},{... | collective-permute-start | bytes 589832 | tf_op jit(solution)/shard_map/ppermute | solution.py:285
  85.0 7.4 %collective-permute-start.21 = (bf16[128,768]{1,0:T(8,128)(2,1)S(1)}, bf16[128,768]{1,0:T(8,128)(2,1)S(1)}, u32[]{:S(2)}, u32[]{:S(2)}) collective-permute-start(bf16[128,768]{1,0:T(8,128)(2,1)S(1)} %shard_map.80.refs_9_), channel_id=1, source_target_pairs={{0,13},{1,14},{2,15},{3,12},{4,9},{5,10},{6,11},{7,8},{8,5},{9,6},... | collective-permute-start | bytes 589832 | tf_op jit(solution)/shard_map/ppermute | solution.py:285
  85.0 10.1 %collective-permute-start.18 = (bf16[128,768]{1,0:T(8,128)(2,1)S(1)}, bf16[128,768]{1,0:T(8,128)(2,1)S(1)}, u32[]{:S(2)}, u32[]{:S(2)}) collective-permute-start(bf16[128,768]{1,0:T(8,128)(2,1)S(1)} %get-tuple-element.26.refs_9_), channel_id=1, source_target_pairs={{0,1},{1,2},{2,3},{3,0},{4,5},{5,6},{6,7},{7,4},{8,9},{9,10},{10,1... | collective-permute-start | bytes 589832 | tf_op jit(solution)/shard_map/ppermute | solution.py:285
  85.1 11.5 %collective-permute-start.17 = (bf16[128,768]{1,0:T(8,128)(2,1)S(1)}, bf16[128,768]{1,0:T(8,128)(2,1)S(1)}, u32[]{:S(2)}, u32[]{:S(2)}) collective-permute-start(bf16[128,768]{1,0:T(8,128)(2,1)S(1)} %get-tuple-element.25), channel_id=1, source_target_pairs={{1,0},{2,1},{3,2},{0,3},{5,4},{6,5},{7,6},{4,7},{9,8},{10,9},{11,1... | collective-permute-start | bytes 589832 | tf_op jit(solution)/shard_map/ppermute | solution.py:288
  (9 other events, 245.5 us)

commit v4 on v3

--- a/solution.py
+++ b/solution.py
@@ -107,7 +107,7 @@
 
 
 def piece_list(width):
-    direct = width // 8
+    direct = width // 4
     pieces = []
     for m, share in ((0, width // 2), (1, (width - direct) // 2)):
         pieces += [(m, r * (share // 3), share // 3, share) for r in range(3)]
@@ -189,11 +189,19 @@
         give(jnp.zeros(x.shape, jnp.bfloat16))
 
 
-def gather_kernel(first_ref, second_ref, own_ref, returned_ref, out_ref):
-    out_ref[0, 0] = first_ref[...]
-    out_ref[0, 1] = second_ref[...]
+def gather_kernel(first_ref, second_ref, own_ref, returned_ref, out_ref, last_ref, sems):
+    rows = (first_ref, second_ref, last_ref)
+    copies = [
+        pltpu.make_async_copy(ref, out_ref.at[0, tick], sems.at[tick])
+        for tick, ref in enumerate(rows)
+    ]
+    copies[0].start()
+    copies[1].start()
     total = own_ref[...].astype(jnp.float32) + returned_ref[...].astype(jnp.float32)
-    out_ref[0, 2] = total.astype(jnp.bfloat16)
+    last_ref[...] = total.astype(jnp.bfloat16)
+    copies[2].start()
+    for copy in copies:
+        copy.wait()
 
 
 def pairs_per_device(
@@ -311,7 +319,11 @@
         gather_kernel,
         out_shape=jax.ShapeDtypeStruct((1, TICKS, num_rows, width), jnp.bfloat16),
         in_specs=[in_vmem] * 4,
-        out_specs=in_vmem,
+        out_specs=anywhere,
+        scratch_shapes=[
+            pltpu.VMEM((num_rows, width), jnp.bfloat16),
+            pltpu.SemaphoreType.DMA((TICKS,)),
+        ],
         compiler_params=limited,
         name="gather",
     )(*outputs, done[0], returned)

time: 104 us -> 105 us (level)
  waiting for transfers between devices: 55.5 us -> 57.2 us
    ppermute x13, waiting for transfers between devices: 28.4 us -> 30 us  [swapped(): lax.ppermute(x, axis, [(i, i ^ 1 << bit) for i in range(lax.axis_size(axi...]
  transfers between devices with their start and end apart: 26 -> 26, of which waited for: 13 -> 12; matrix products, arithmetic and copies ran while one was open for 0% -> 0% of each run, Pallas kernels for 8% -> 8%
where the time goes in v4:
time: 105 us
  waiting for transfers between devices  57.2 us (54%)
  starting transfers between devices  35.3 us (34%)
  Pallas kernels  11.9 us (11%)
    ppermute x13, waiting for transfers between devices, swapped(): lax.ppermute(x, axis, [(i, i ^ 1 << bit) for i in range(lax.axis_size(axi...  30 us
    ppermute x8, starting transfers between devices, ahead(): return lax.ppermute(value, ('expert', 'section'), perm)  23 us
    ppermute x8, waiting for transfers between devices, ahead(): return lax.ppermute(value, ('expert', 'section'), perm)  21.3 us
    pallas_call x6, Pallas kernels, layer(): pl.pallas_call(functools.partial(layer_kernel, tick, which, TICKS - 1), o...  7.93 us
    ppermute x13, starting transfers between devices, swapped(): lax.ppermute(x, axis, [(i, i ^ 1 << bit) for i in range(lax.axis_size(axi...  7.8 us
    ppermute x2, waiting for transfers between devices, back(): lax.ppermute(value, 'section', [((s + 1) % legs, s) for s in range(legs)])  5.55 us
    ppermute x2, starting transfers between devices, pairs_per_device(): lax.ppermute(own_rows, 'expert', [(e, places - 1 - e) for e in senders])  3.87 us
    pallas_call x2, Pallas kernels, cut(): pl.pallas_call(functools.partial(cut_kernel, some), out_shape=[pltpu.VMEM...  2.35 us
  transfers between devices with their start and end apart: 26, of which 12 were waited for; matrix products, arithmetic and copies ran while one was open for 0% of the time, Pallas kernels for 8%

profile of v4, /device:TPU:13, one launch (start us, length us, event | category | flops | bytes accessed | tf_op | source)
XLA Modules:
  0.0 104.7 jit_solution(5850271983782103420)
XLA Ops:
  0.0 1.4 %shard_map.74 = (bf16[128,768]{1,0:T(8,128)(2,1)S(1)}, bf16[128,768]{1,0:T(8,128)(2,1)S(1)}, bf16[96,768]{1,0:T(8,128)(2,1)S(1)}, bf16[96,768]{1,0:T(8,128)(2,1)...) custom-call(bf16[768,768]{1,0:T(8,128)(2,1)} %bitcast.6, bf16[768,768]{1,0:T(8,128)(2,1)} %bitcast.15), custom_call_target="tpu_custom_call" | custom-call | tf_op jit(solution)/shard_map/pallas_call | solution.py:227
  1.7 1.4 %collective-permute-start.8 = (bf16[96,768]{1,0:T(8,128)(2,1)S(1)}, bf16[96,768]{1,0:T(8,128)(2,1)S(1)}, u32[]{:S(2)}, u32[]{:S(2)}) collective-permute-start(bf16[96,768]{1,0:T(8,128)(2,1)S(1)} %get-tuple-element.21), channel_id=1, source_target_pairs={{0,4},{4,0},{8,12},{12,8},{1,5},{5,1},{9,13},{13,9},{2,6},{6,2},{1... | collective-permute-start | bytes 442376 | tf_op jit(solution)/shard_map/ppermute | solution.py:15
  7.0 2.4 %collective-permute-done.8.refs_2_ = bf16[96,768]{1,0:T(8,128)(2,1)S(1)} collective-permute-done((bf16[96,768]{1,0:T(8,128)(2,1)S(1)}, bf16[96,768]{1,0:T(8,128)(2,1)S(1)}, u32[]{:S(2)}, u32[]{:S(2)}) %collective-permute-start.8) | collective-permute-done | bytes 147488 | tf_op jit(solution)/shard_map/ppermute | solution.py:15
  9.6 11.4 %collective-permute-done.10.refs_4_ = bf16[96,768]{1,0:T(8,128)(2,1)S(1)} collective-permute-done((bf16[96,768]{1,0:T(8,128)(2,1)S(1)}, bf16[96,768]{1,0:T(8,128)(2,1)S(1)}, u32[]{:S(2)}, u32[]{:S(2)}) %collective-permute-start.10) | collective-permute-done | bytes 147488 | tf_op jit(solution)/shard_map/ppermute | solution.py:15
  21.2 1.2 %collective-permute-start.9 = (bf16[96,768]{1,0:T(8,128)(2,1)S(1)}, bf16[96,768]{1,0:T(8,128)(2,1)S(1)}, u32[]{:S(2)}, u32[]{:S(2)}) collective-permute-start(bf16[96,768]{1,0:T(8,128)(2,1)S(1)} %collective-permute-done.8.refs_2_), channel_id=1, source_target_pairs={{0,16},{16,0},{1,17},{17,1},{2,18},{18,2},{3,19},{19,3},{4,20},{20... | collective-permute-start | bytes 442376 | tf_op jit(solution)/shard_map/ppermute | solution.py:15
  22.7 8.8 %collective-permute-done.4.refs_4_ = bf16[128,768]{1,0:T(8,128)(2,1)S(1)} collective-permute-done((bf16[128,768]{1,0:T(8,128)(2,1)S(1)}, bf16[128,768]{1,0:T(8,128)(2,1)S(1)}, u32[]{:S(2)}, u32[]{:S(2)}) %collective-permute-start.4) | collective-permute-done | bytes 196640 | tf_op jit(solution)/shard_map/ppermute | solution.py:15
  33.2 3.2 %collective-permute-start.14 = (bf16[128,768]{1,0:T(8,128)(2,1)S(1)}, bf16[128,768]{1,0:T(8,128)(2,1)S(1)}, u32[]{:S(2)}, u32[]{:S(2)}) collective-permute-start(bf16[128,768]{1,0:T(8,128)(2,1)S(1)} %bitcast.24), channel_id=1, source_target_pairs={{4,8},{8,4},{5,9},{9,5},{6,10},{10,6},{7,11},{11,7},{20,24},{24,20... | collective-permute-start | bytes 589832 | tf_op jit(solution)/shard_map/ppermute | solution.py:269
  37.9 2.8 %collective-permute-done.3.refs_3_ = bf16[128,768]{1,0:T(8,128)(2,1)S(1)} collective-permute-done((bf16[128,768]{1,0:T(8,128)(2,1)S(1)}, bf16[128,768]{1,0:T(8,128)(2,1)S(1)}, u32[]{:S(2)}, u32[]{:S(2)}) %collective-permute-start.3) | collective-permute-done | bytes 196640 | tf_op jit(solution)/shard_map/ppermute | solution.py:15
  40.6 4.2 %collective-permute-done.5.refs_5_ = bf16[128,768]{1,0:T(8,128)(2,1)S(1)} collective-permute-done((bf16[128,768]{1,0:T(8,128)(2,1)S(1)}, bf16[128,768]{1,0:T(8,128)(2,1)S(1)}, u32[]{:S(2)}, u32[]{:S(2)}) %collective-permute-start.5) | collective-permute-done | bytes 196640 | tf_op jit(solution)/shard_map/ppermute | solution.py:15
  45.0 1.3 %shard_map.77.refs_9_ = bf16[128,768]{1,0:T(8,128)(2,1)S(1)} custom-call(s32[8,128]{1,0:T(8,128)S(1)} %mask.1.refs_0_, bf16[128,768]{1,0:T(8,128)(2,1)S(1)} %collective-permute-done.13.refs_1_, bf16[128,768]{1,0:T(8,128)(2,1)S(1)} %collective-permute-done.14.refs_2_, f32[1,768]{1,0:T(1,128)S(1)} %copy-done.4, bf16[2,768]{1,0:T(2,128)(2,1)S(1)} %bitcast.29, ...), custom_call_target="tpu_custom_call" | custom-call | tf_op jit(solution)/shard_map/pallas_call | solution.py:278
  46.3 3.4 %collective-permute-start.16 = (bf16[128,768]{1,0:T(8,128)(2,1)S(1)}, bf16[128,768]{1,0:T(8,128)(2,1)S(1)}, u32[]{:S(2)}, u32[]{:S(2)}) collective-permute-start(bf16[128,768]{1,0:T(8,128)(2,1)S(1)} %shard_map.77.refs_9_), channel_id=1, source_target_pairs={{0,13},{1,14},{2,15},{3,12},{4,9},{5,10},{6,11},{7,8},{8,5},{9,6},... | collective-permute-start | bytes 589832 | tf_op jit(solution)/shard_map/ppermute | solution.py:293
  49.7 1.3 %shard_map.78 = (bf16[128,768]{1,0:T(8,128)(2,1)S(1)}, bf16[128,768]{1,0:T(8,128)(2,1)S(1)}) custom-call(s32[8,128]{1,0:T(8,128)S(1)} %mask.1.refs_0_, bf16[128,768]{1,0:T(8,128)(2,1)S(1)} %bitcast.27, bf16[2,128,768]{2,1,0:T(8,128)(2,1)S(1)} %copy-done.2, f32[1,768]{1,0:T(1,128)S(1)} %copy-done.4, bf16[2,768]{1,0:T(2,128)(2,1)S(1)} %bitcast.30, ...), custom_call_target="tpu_custom_call" | custom-call | tf_op jit(solution)/shard_map/pallas_call | solution.py:278
  51.2 3.5 %collective-permute-start.19 = (bf16[128,768]{1,0:T(8,128)(2,1)S(1)}, bf16[128,768]{1,0:T(8,128)(2,1)S(1)}, u32[]{:S(2)}, u32[]{:S(2)}) collective-permute-start(bf16[128,768]{1,0:T(8,128)(2,1)S(1)} %shard_map.77.refs_9_), channel_id=1, source_target_pairs={{0,1},{1,2},{2,3},{4,5},{5,6},{6,7},{8,9},{9,10},{10,11},{12,13},{... | collective-permute-start | bytes 589832 | tf_op jit(solution)/shard_map/ppermute | solution.py:293
  54.8 11.6 %collective-permute-done.16.refs_2_ = bf16[128,768]{1,0:T(8,128)(2,1)S(1)} collective-permute-done((bf16[128,768]{1,0:T(8,128)(2,1)S(1)}, bf16[128,768]{1,0:T(8,128)(2,1)S(1)}, u32[]{:S(2)}, u32[]{:S(2)}) %collective-permute-start.16) | collective-permute-done | bytes 196640 | tf_op jit(solution)/shard_map/ppermute | solution.py:293
  66.5 1.3 %shard_map.79 = (bf16[128,768]{1,0:T(8,128)(2,1)S(1)}, bf16[128,768]{1,0:T(8,128)(2,1)S(1)}, bf16[128,768]{1,0:T(8,128)(2,1)S(1)}) custom-call(s32[8,128]{1,0:T(8,128)S(1)} %mask.1.refs_0_, bf16[128,768]{1,0:T(8,128)(2,1)S(1)} %collective-permute-done.15.refs_1_, bf16[128,768]{1,0:T(8,128)(2,1)S(1)} %collective-permute-done.16.refs_2_, ...), custom_call_target="tpu_custom_call" | custom-call | tf_op jit(solution)/shard_map/pallas_call | solution.py:278
  67.8 2.3 %collective-permute-start.23 = (bf16[128,768]{1,0:T(8,128)(2,1)S(1)}, bf16[128,768]{1,0:T(8,128)(2,1)S(1)}, u32[]{:S(2)}, u32[]{:S(2)}) collective-permute-start(bf16[128,768]{1,0:T(8,128)(2,1)S(1)} %get-tuple-element.28), channel_id=1, source_target_pairs={{0,13},{1,14},{2,15},{3,12},{4,9},{5,10},{6,11},{7,8},{8,5},{9,6},... | collective-permute-start | bytes 589832 | tf_op jit(solution)/shard_map/ppermute | solution.py:293
  70.2 1.5 %collective-permute-done.20.refs_2_ = bf16[128,768]{1,0:T(8,128)(2,1)S(1)} collective-permute-done((bf16[128,768]{1,0:T(8,128)(2,1)S(1)}, bf16[128,768]{1,0:T(8,128)(2,1)S(1)}, u32[]{:S(2)}, u32[]{:S(2)}) %collective-permute-start.20) | collective-permute-done | bytes 196640 | tf_op jit(solution)/shard_map/ppermute | solution.py:293
  71.7 1.3 %shard_map.80.refs_9_ = bf16[128,768]{1,0:T(8,128)(2,1)S(1)} custom-call(s32[8,128]{1,0:T(8,128)S(1)} %mask.1.refs_0_, bf16[128,768]{1,0:T(8,128)(2,1)S(1)} %collective-permute-done.19.refs_1_, bf16[128,768]{1,0:T(8,128)(2,1)S(1)} %collective-permute-done.20.refs_2_, f32[1,768]{1,0:T(1,128)S(1)} %copy-done.4, bf16[2,768]{1,0:T(2,128)(2,1)S(1)} %bitcast.32, ...), custom_call_target="tpu_custom_call" | custom-call | tf_op jit(solution)/shard_map/pallas_call | solution.py:278
  73.0 13.4 %collective-permute-start.22 = (bf16[128,768]{1,0:T(8,128)(2,1)S(1)}, bf16[128,768]{1,0:T(8,128)(2,1)S(1)}, u32[]{:S(2)}, u32[]{:S(2)}) collective-permute-start(bf16[128,768]{1,0:T(8,128)(2,1)S(1)} %shard_map.80.refs_9_), channel_id=1, source_target_pairs={{0,1},{1,2},{2,3},{4,5},{5,6},{6,7},{8,9},{9,10},{10,11},{12,13},{... | collective-permute-start | bytes 589832 | tf_op jit(solution)/shard_map/ppermute | solution.py:293
  87.0 5.3 %collective-permute-done.22.refs_1_ = bf16[128,768]{1,0:T(8,128)(2,1)S(1)} collective-permute-done((bf16[128,768]{1,0:T(8,128)(2,1)S(1)}, bf16[128,768]{1,0:T(8,128)(2,1)S(1)}, u32[]{:S(2)}, u32[]{:S(2)}) %collective-permute-start.22) | collective-permute-done | bytes 196640 | tf_op jit(solution)/shard_map/ppermute | solution.py:293
  92.4 1.3 %shard_map.81.refs_10_ = bf16[128,768]{1,0:T(8,128)(2,1)S(1)} custom-call(s32[8,128]{1,0:T(8,128)S(1)} %mask.1.refs_0_, bf16[128,768]{1,0:T(8,128)(2,1)S(1)} %collective-permute-done.22.refs_1_, bf16[128,768]{1,0:T(8,128)(2,1)S(1)} %collective-permute-done.23.refs_2_, f32[1,768]{1,0:T(1,128)S(1)} %copy-done.4, bf16[2,768]{1,0:T(2,128)(2,1)S(1)} %bitcast.33, ...), custom_call_target="tpu_custom_call" | custom-call | tf_op jit(solution)/shard_map/pallas_call | solution.py:278
  93.8 2.8 %collective-permute-done.18.refs_1_ = bf16[128,768]{1,0:T(8,128)(2,1)S(1)} collective-permute-done((bf16[128,768]{1,0:T(8,128)(2,1)S(1)}, bf16[128,768]{1,0:T(8,128)(2,1)S(1)}, u32[]{:S(2)}, u32[]{:S(2)}) %collective-permute-start.18) | collective-permute-done | bytes 196640 | tf_op jit(solution)/shard_map/ppermute | solution.py:293
  96.6 1.3 %shard_map.82 = (bf16[128,768]{1,0:T(8,128)(2,1)S(1)}, bf16[128,768]{1,0:T(8,128)(2,1)S(1)}) custom-call(s32[8,128]{1,0:T(8,128)S(1)} %mask.1.refs_0_, bf16[128,768]{1,0:T(8,128)(2,1)S(1)} %collective-permute-done.18.refs_1_, bf16[128,768]{1,0:T(8,128)(2,1)S(1)} %collective-permute-done.21.refs_2_, bf16[2,128,768]{2,1,0:T(8,128)(2,1)S(1)} %copy-done.2, ...), custom_call_target="tpu_custom_call" | custom-call | tf_op jit(solution)/shard_map/pallas_call | solution.py:278
  98.3 5.5 %collective-permute-done.24.second_ref = bf16[128,768]{1,0:T(8,128)(2,1)S(1)} collective-permute-done((bf16[128,768]{1,0:T(8,128)(2,1)S(1)}, bf16[128,768]{1,0:T(8,128)(2,1)S(1)}, u32[]{:S(2)}, u32[]{:S(2)}) %collective-permute-start.24) | collective-permute-done | bytes 196640 | tf_op jit(solution)/shard_map/ppermute | solution.py:296
  (54 shorter events, 10.1 us)
Async XLA Ops:
  1.7 7.7 %collective-permute-start.8 = (bf16[96,768]{1,0:T(8,128)(2,1)S(1)}, bf16[96,768]{1,0:T(8,128)(2,1)S(1)}, u32[]{:S(2)}, u32[]{:S(2)}) collective-permute-start(bf16[96,768]{1,0:T(8,128)(2,1)S(1)} %get-tuple-element.21), channel_id=1, source_target_pairs={{0,4},{4,0},{8,12},{12,8},{1,5},{5,1},{9,13},{13,9},{2,6},{6,2},{1... | collective-permute-start | bytes 442376 | tf_op jit(solution)/shard_map/ppermute | solution.py:15
  4.0 17.2 %collective-permute-start = (bf16[128,768]{1,0:T(8,128)(2,1)S(1)}, bf16[128,768]{1,0:T(8,128)(2,1)S(1)}, u32[]{:S(2)}, u32[]{:S(2)}) collective-permute-start(bf16[128,768]{1,0:T(8,128)(2,1)S(1)} %shard_map.73), channel_id=1, source_target_pairs={{0,4},{4,0},{8,12},{12,8},{1,5},{5,1},{9,13},{13,9},{2,6},{6,2},{1... | collective-permute-start | bytes 589832 | tf_op jit(solution)/shard_map/ppermute | solution.py:15
  4.4 18.0 %collective-permute-start.2 = (bf16[128,768]{1,0:T(8,128)(2,1)S(1)}, bf16[128,768]{1,0:T(8,128)(2,1)S(1)}, u32[]{:S(2)}, u32[]{:S(2)}) collective-permute-start(bf16[128,768]{1,0:T(8,128)(2,1)S(1)} %get-tuple-element.18), channel_id=1, source_target_pairs={{0,4},{4,0},{8,12},{12,8},{1,5},{5,1},{9,13},{13,9},{2,6},{6,2},{1... | collective-permute-start | bytes 589832 | tf_op jit(solution)/shard_map/ppermute | solution.py:15
  5.5 15.4 %collective-permute-start.10 = (bf16[96,768]{1,0:T(8,128)(2,1)S(1)}, bf16[96,768]{1,0:T(8,128)(2,1)S(1)}, u32[]{:S(2)}, u32[]{:S(2)}) collective-permute-start(bf16[96,768]{1,0:T(8,128)(2,1)S(1)} %get-tuple-element.22), channel_id=1, source_target_pairs={{0,4},{4,0},{8,12},{12,8},{1,5},{5,1},{9,13},{13,9},{2,6},{6,2},{1... | collective-permute-start | bytes 442376 | tf_op jit(solution)/shard_map/ppermute | solution.py:15
  6.2 30.2 %collective-permute-start.12 = (bf16[192,768]{1,0:T(8,128)(2,1)S(1)}, bf16[192,768]{1,0:T(8,128)(2,1)S(1)}, u32[]{:S(2)}, u32[]{:S(2)}) collective-permute-start(bf16[192,768]{1,0:T(8,128)(2,1)S(1)} %get-tuple-element.23), channel_id=1, source_target_pairs={{0,4},{4,0},{8,12},{12,8},{1,5},{5,1},{9,13},{13,9},{2,6},{6,2},{1... | collective-permute-start | bytes 884744 | tf_op jit(solution)/shard_map/ppermute | solution.py:15
  9.4 22.1 %collective-permute-start.4 = (bf16[128,768]{1,0:T(8,128)(2,1)S(1)}, bf16[128,768]{1,0:T(8,128)(2,1)S(1)}, u32[]{:S(2)}, u32[]{:S(2)}) collective-permute-start(bf16[128,768]{1,0:T(8,128)(2,1)S(1)} %get-tuple-element.19), channel_id=1, source_target_pairs={{0,4},{4,0},{8,12},{12,8},{1,5},{5,1},{9,13},{13,9},{2,6},{6,2},{1... | collective-permute-start | bytes 589832 | tf_op jit(solution)/shard_map/ppermute | solution.py:15
  21.0 10.8 %collective-permute-start.7 = (bf16[96,768]{1,0:T(8,128)(2,1)S(1)}, bf16[96,768]{1,0:T(8,128)(2,1)S(1)}, u32[]{:S(2)}, u32[]{:S(2)}) collective-permute-start(bf16[96,768]{1,0:T(8,128)(2,1)S(1)} %collective-permute-done.6.refs_0_), channel_id=1, source_target_pairs={{0,16},{16,0},{1,17},{17,1},{2,18},{18,2},{3,19},{19,3},{4,20},{20... | collective-permute-start | bytes 442376 | tf_op jit(solution)/shard_map/ppermute | solution.py:15
  21.2 11.8 %collective-permute-start.9 = (bf16[96,768]{1,0:T(8,128)(2,1)S(1)}, bf16[96,768]{1,0:T(8,128)(2,1)S(1)}, u32[]{:S(2)}, u32[]{:S(2)}) collective-permute-start(bf16[96,768]{1,0:T(8,128)(2,1)S(1)} %collective-permute-done.8.refs_2_), channel_id=1, source_target_pairs={{0,16},{16,0},{1,17},{17,1},{2,18},{18,2},{3,19},{19,3},{4,20},{20... | collective-permute-start | bytes 442376 | tf_op jit(solution)/shard_map/ppermute | solution.py:15
  22.4 10.8 %collective-permute-start.11 = (bf16[96,768]{1,0:T(8,128)(2,1)S(1)}, bf16[96,768]{1,0:T(8,128)(2,1)S(1)}, u32[]{:S(2)}, u32[]{:S(2)}) collective-permute-start(bf16[96,768]{1,0:T(8,128)(2,1)S(1)} %collective-permute-done.10.refs_4_), channel_id=1, source_target_pairs={{0,16},{16,0},{1,17},{17,1},{2,18},{18,2},{3,19},{19,3},{4,20},{20... | collective-permute-start | bytes 442376 | tf_op jit(solution)/shard_map/ppermute | solution.py:15
  31.5 6.4 %collective-permute-start.1 = (bf16[128,768]{1,0:T(8,128)(2,1)S(1)}, bf16[128,768]{1,0:T(8,128)(2,1)S(1)}, u32[]{:S(2)}, u32[]{:S(2)}) collective-permute-start(bf16[128,768]{1,0:T(8,128)(2,1)S(1)} %collective-permute-done.refs_0_), channel_id=1, source_target_pairs={{0,16},{16,0},{1,17},{17,1},{2,18},{18,2},{3,19},{19,3},{4,20},{20... | collective-permute-start | bytes 589832 | tf_op jit(solution)/shard_map/ppermute | solution.py:15
  31.7 8.9 %collective-permute-start.3 = (bf16[128,768]{1,0:T(8,128)(2,1)S(1)}, bf16[128,768]{1,0:T(8,128)(2,1)S(1)}, u32[]{:S(2)}, u32[]{:S(2)}) collective-permute-start(bf16[128,768]{1,0:T(8,128)(2,1)S(1)} %collective-permute-done.2.refs_2_), channel_id=1, source_target_pairs={{0,16},{16,0},{1,17},{17,1},{2,18},{18,2},{3,19},{19,3},{4,20},{20... | collective-permute-start | bytes 589832 | tf_op jit(solution)/shard_map/ppermute | solution.py:15
  33.0 11.9 %collective-permute-start.5 = (bf16[128,768]{1,0:T(8,128)(2,1)S(1)}, bf16[128,768]{1,0:T(8,128)(2,1)S(1)}, u32[]{:S(2)}, u32[]{:S(2)}) collective-permute-start(bf16[128,768]{1,0:T(8,128)(2,1)S(1)} %collective-permute-done.4.refs_4_), channel_id=1, source_target_pairs={{0,16},{16,0},{1,17},{17,1},{2,18},{18,2},{3,19},{19,3},{4,20},{20... | collective-permute-start | bytes 589832 | tf_op jit(solution)/shard_map/ppermute | solution.py:15
  33.2 11.7 %collective-permute-start.14 = (bf16[128,768]{1,0:T(8,128)(2,1)S(1)}, bf16[128,768]{1,0:T(8,128)(2,1)S(1)}, u32[]{:S(2)}, u32[]{:S(2)}) collective-permute-start(bf16[128,768]{1,0:T(8,128)(2,1)S(1)} %bitcast.24), channel_id=1, source_target_pairs={{4,8},{8,4},{5,9},{9,5},{6,10},{10,6},{7,11},{11,7},{20,24},{24,20... | collective-permute-start | bytes 589832 | tf_op jit(solution)/shard_map/ppermute | solution.py:269
  36.4 8.5 %collective-permute-start.13 = (bf16[128,768]{1,0:T(8,128)(2,1)S(1)}, bf16[128,768]{1,0:T(8,128)(2,1)S(1)}, u32[]{:S(2)}, u32[]{:S(2)}) collective-permute-start(bf16[128,768]{1,0:T(8,128)(2,1)S(1)} %bitcast.25), channel_id=1, source_target_pairs={{0,12},{12,0},{1,13},{13,1},{2,14},{14,2},{3,15},{15,3},{16,28},{2... | collective-permute-start | bytes 589832 | tf_op jit(solution)/shard_map/ppermute | solution.py:269
  46.3 20.2 %collective-permute-start.16 = (bf16[128,768]{1,0:T(8,128)(2,1)S(1)}, bf16[128,768]{1,0:T(8,128)(2,1)S(1)}, u32[]{:S(2)}, u32[]{:S(2)}) collective-permute-start(bf16[128,768]{1,0:T(8,128)(2,1)S(1)} %shard_map.77.refs_9_), channel_id=1, source_target_pairs={{0,13},{1,14},{2,15},{3,12},{4,9},{5,10},{6,11},{7,8},{8,5},{9,6},... | collective-permute-start | bytes 589832 | tf_op jit(solution)/shard_map/ppermute | solution.py:293
  51.1 15.4 %collective-permute-start.15 = (bf16[128,768]{1,0:T(8,128)(2,1)S(1)}, bf16[128,768]{1,0:T(8,128)(2,1)S(1)}, u32[]{:S(2)}, u32[]{:S(2)}) collective-permute-start(bf16[128,768]{1,0:T(8,128)(2,1)S(1)} %get-tuple-element.24.refs_10_), channel_id=1, source_target_pairs={{0,1},{1,2},{2,3},{3,0},{4,5},{5,6},{6,7},{7,4},{8,9},{9,10},{10,1... | collective-permute-start | bytes 589832 | tf_op jit(solution)/shard_map/ppermute | solution.py:293
  51.2 19.0 %collective-permute-start.19 = (bf16[128,768]{1,0:T(8,128)(2,1)S(1)}, bf16[128,768]{1,0:T(8,128)(2,1)S(1)}, u32[]{:S(2)}, u32[]{:S(2)}) collective-permute-start(bf16[128,768]{1,0:T(8,128)(2,1)S(1)} %shard_map.77.refs_9_), channel_id=1, source_target_pairs={{0,1},{1,2},{2,3},{4,5},{5,6},{6,7},{8,9},{9,10},{10,11},{12,13},{... | collective-permute-start | bytes 589832 | tf_op jit(solution)/shard_map/ppermute | solution.py:293
  54.8 16.9 %collective-permute-start.20 = (bf16[128,768]{1,0:T(8,128)(2,1)S(1)}, bf16[128,768]{1,0:T(8,128)(2,1)S(1)}, u32[]{:S(2)}, u32[]{:S(2)}) collective-permute-start(bf16[128,768]{1,0:T(8,128)(2,1)S(1)} %get-tuple-element.27), channel_id=1, source_target_pairs={{0,13},{1,14},{2,15},{3,12},{4,9},{5,10},{6,11},{7,8},{8,5},{9,6},... | collective-permute-start | bytes 589832 | tf_op jit(solution)/shard_map/ppermute | solution.py:293
  67.8 19.2 %collective-permute-start.23 = (bf16[128,768]{1,0:T(8,128)(2,1)S(1)}, bf16[128,768]{1,0:T(8,128)(2,1)S(1)}, u32[]{:S(2)}, u32[]{:S(2)}) collective-permute-start(bf16[128,768]{1,0:T(8,128)(2,1)S(1)} %get-tuple-element.28), channel_id=1, source_target_pairs={{0,13},{1,14},{2,15},{3,12},{4,9},{5,10},{6,11},{7,8},{8,5},{9,6},... | collective-permute-start | bytes 589832 | tf_op jit(solution)/shard_map/ppermute | solution.py:293
  73.0 19.3 %collective-permute-start.22 = (bf16[128,768]{1,0:T(8,128)(2,1)S(1)}, bf16[128,768]{1,0:T(8,128)(2,1)S(1)}, u32[]{:S(2)}, u32[]{:S(2)}) collective-permute-start(bf16[128,768]{1,0:T(8,128)(2,1)S(1)} %shard_map.80.refs_9_), channel_id=1, source_target_pairs={{0,1},{1,2},{2,3},{4,5},{5,6},{6,7},{8,9},{9,10},{10,11},{12,13},{... | collective-permute-start | bytes 589832 | tf_op jit(solution)/shard_map/ppermute | solution.py:293
  86.4 7.4 %collective-permute-start.21 = (bf16[128,768]{1,0:T(8,128)(2,1)S(1)}, bf16[128,768]{1,0:T(8,128)(2,1)S(1)}, u32[]{:S(2)}, u32[]{:S(2)}) collective-permute-start(bf16[128,768]{1,0:T(8,128)(2,1)S(1)} %shard_map.80.refs_9_), channel_id=1, source_target_pairs={{0,13},{1,14},{2,15},{3,12},{4,9},{5,10},{6,11},{7,8},{8,5},{9,6},... | collective-permute-start | bytes 589832 | tf_op jit(solution)/shard_map/ppermute | solution.py:293
  86.5 10.1 %collective-permute-start.18 = (bf16[128,768]{1,0:T(8,128)(2,1)S(1)}, bf16[128,768]{1,0:T(8,128)(2,1)S(1)}, u32[]{:S(2)}, u32[]{:S(2)}) collective-permute-start(bf16[128,768]{1,0:T(8,128)(2,1)S(1)} %get-tuple-element.26.refs_9_), channel_id=1, source_target_pairs={{0,1},{1,2},{2,3},{3,0},{4,5},{5,6},{6,7},{7,4},{8,9},{9,10},{10,1... | collective-permute-start | bytes 589832 | tf_op jit(solution)/shard_map/ppermute | solution.py:293
  86.5 11.5 %collective-permute-start.17 = (bf16[128,768]{1,0:T(8,128)(2,1)S(1)}, bf16[128,768]{1,0:T(8,128)(2,1)S(1)}, u32[]{:S(2)}, u32[]{:S(2)}) collective-permute-start(bf16[128,768]{1,0:T(8,128)(2,1)S(1)} %get-tuple-element.25), channel_id=1, source_target_pairs={{1,0},{2,1},{3,2},{0,3},{5,4},{6,5},{7,6},{4,7},{9,8},{10,9},{11,1... | collective-permute-start | bytes 589832 | tf_op jit(solution)/shard_map/ppermute | solution.py:296
  97.9 5.9 %collective-permute-start.24 = (bf16[128,768]{1,0:T(8,128)(2,1)S(1)}, bf16[128,768]{1,0:T(8,128)(2,1)S(1)}, u32[]{:S(2)}, u32[]{:S(2)}) collective-permute-start(bf16[128,768]{1,0:T(8,128)(2,1)S(1)} %get-tuple-element.29), channel_id=1, source_target_pairs={{1,0},{2,1},{3,2},{0,3},{5,4},{6,5},{7,6},{4,7},{9,8},{10,9},{11,1... | collective-permute-start | bytes 589832 | tf_op jit(solution)/shard_map/ppermute | solution.py:296
  (9 other events, 255.4 us)
